TPU v7x, 512 devices: a whole 4x4x16 slice. The times are simulated.
512 devices in a mesh: pool: 32 (over z, y_hi), band: 16 (over y_lo, x, core).
Axes of the slice: x: 4, y: 4 (y_hi: 2, y_lo: 2; y = y_hi * 2 + y_lo), z: 16, core: 2. Of those that a mesh axis runs over, the one named last changes fastest.
Arguments:
- orbitals: bfloat16 [32, 16, 2, 46656], P('pool', 'band'), may hold values from -6 to 6
- occupation: int32 [32, 16], P('pool', 'band'), may hold values from 1 to 2
- kernel: float32 [46656], replicated, may hold values from 0.02 to 2
Outputs:
- exchanged: bfloat16 [32, 16, 2, 46656], P('pool', 'band')
- gram_matrix: float32 [32, 2, 16, 16], P('pool', None, None, 'band')
All inputs are finite; a program needn't handle non-finite values.
Results may differ from a plain program's by a relative error of at most 0.013.
Values may be sent and summed in bfloat16 or wider, within the bound.
A program may use at most 64 MiB of HBM per device.

v0:
```python
import math

import jax
import jax.numpy as jnp
from jax import lax
from jax.sharding import PartitionSpec as P

NG = 36
GRID = 46656


def shifted(array, axis, by):
    length = lax.axis_size(axis)
    return lax.ppermute(array, axis, [(i, (i + by) % length) for i in range(length)])


def dft_matrix(direction):
    points = jnp.arange(NG, dtype=jnp.int32)
    phases = points[:, None] * points[None, :] % NG
    angles = 2.0 * math.pi / NG * phases.astype(jnp.float32)
    cosine = jnp.cos(angles)
    sine = direction * jnp.sin(angles)
    blocks = jnp.stack([jnp.stack([cosine, sine]), jnp.stack([-sine, cosine])])
    return jnp.transpose(blocks, (0, 2, 1, 3)).astype(jnp.bfloat16)


def transform(values, matrix, keep_float):
    count = values.shape[0]
    current = values.reshape(count, 2, NG, NG * NG)
    product = jnp.einsum("uavb,pvbc->puac", matrix, current, preferred_element_type=jnp.float32)
    current = product.astype(jnp.bfloat16).reshape(count, 2, NG, NG, NG)
    product = jnp.einsum("uavb,pvxbz->puxaz", matrix, current, preferred_element_type=jnp.float32)
    current = product.astype(jnp.bfloat16)
    product = jnp.einsum("uavb,pvxyb->puxya", matrix, current, preferred_element_type=jnp.float32)
    if not keep_float:
        product = product.astype(jnp.bfloat16)
    return product.reshape(count, 2, NG * NG * NG)


def add_block(
    accum_real,
    accum_imag,
    local_bands,
    visiting,
    visiting_occ,
    kernel,
    forward_matrix,
    inverse_matrix,
):
    c = local_bands[:, 0].astype(jnp.float32)[None]
    d = local_bands[:, 1].astype(jnp.float32)[None]
    a = visiting[:, 0].astype(jnp.float32)[:, None]
    b = visiting[:, 1].astype(jnp.float32)[:, None]
    visits = visiting.shape[0]
    owned = local_bands.shape[0]
    density = jnp.stack([a * c + b * d, a * d - b * c], axis=2).astype(jnp.bfloat16)
    density = density.reshape(visits * owned, 2, density.shape[3])
    spectrum = transform(density, forward_matrix, False)
    screened = (spectrum.astype(jnp.float32) * (kernel / GRID)).astype(jnp.bfloat16)
    potential = transform(screened, inverse_matrix, True)
    potential = potential.reshape(visits, owned, 2, potential.shape[2])
    weight = (-0.5 * visiting_occ.astype(jnp.float32))[:, None, None]
    e = potential[:, :, 0]
    f = potential[:, :, 1]
    accum_real = accum_real + jnp.sum(weight * (a * e - b * f), axis=0)
    accum_imag = accum_imag + jnp.sum(weight * (a * f + b * e), axis=0)
    return (accum_real, accum_imag)


def contract(x, y):
    return jnp.einsum("ig,jg->ij", x, y, preferred_element_type=jnp.float32)


def gram_block(bra_rows, ket_rows):
    c = bra_rows[:, 0]
    d = bra_rows[:, 1]
    e = ket_rows[:, 0]
    f = ket_rows[:, 1]
    real_part = contract(c, e) + contract(d, f)
    imag_part = contract(c, f) - contract(d, e)
    return jnp.stack([real_part, imag_part])


def shards(orbitals, occupation, kernel):
    local_bands = orbitals[0]
    own_occupation = occupation[0]
    forward_matrix = dft_matrix(1.0)
    inverse_matrix = dft_matrix(-1.0)
    zeros_grid = jnp.zeros((local_bands.shape[0], local_bands.shape[2]), jnp.float32)
    first_block, first_occ = shifted((local_bands, own_occupation), "pool", 1)
    accum_real, accum_imag = add_block(
        zeros_grid,
        zeros_grid,
        local_bands,
        first_block,
        first_occ,
        kernel,
        forward_matrix,
        inverse_matrix,
    )
    second_block, second_occ = shifted((first_block, first_occ), "band", 1)
    accum_real, accum_imag = add_block(
        accum_real,
        accum_imag,
        local_bands,
        second_block,
        second_occ,
        kernel,
        forward_matrix,
        inverse_matrix,
    )
    exchanged = jnp.stack([accum_real, accum_imag], axis=1).astype(jnp.bfloat16)
    norm_factor = 1.0 / math.sqrt(GRID)
    part = (
        gram_block(lax.all_gather(local_bands, "band", axis=0, tiled=True), exchanged) * norm_factor
    )
    return (exchanged[None], part[None])


def solution(mesh):
    return jax.shard_map(
        shards,
        mesh=mesh,
        in_specs=(P("pool", "band", None, None), P("pool", "band"), P()),
        out_specs=(P("pool", "band", None, None), P("pool", None, None, "band")),
        check_vma=False,
    )
```

profile of v0, /device:TPU:1, one launch (start us, length us, event | category | flops | bytes accessed | tf_op | source)
XLA Modules:
  0.0 71.4 jit_solution(13063176755829954966)
XLA Ops:
  7.2 0.0 all-gather.3.cloned.1.call-start
  7.2 0.7 all-gather.3.cloned.1.call-update
  7.9 5.6 %collective-permute-start.1 = (bf16[1,2,46656]{2,1,0:T(2,128)(2,1)}, bf16[1,2,46656]{2,1,0:T(2,128)(2,1)S(1)}, u32[]{:S(2)}, u32[]{:S(2)}) collective-permute-start(bf16[1,2,46656]{2,1,0:T(2,128)(2,1)} %bitcast.325), channel_id=1, source_target_pairs={{0,16},{16,32},{32,48},{48,64},{64,80},{80,96},{96,112},{112,128},... | collective-permute-start | bytes 559880 | tf_op jit(solution)/shard_map/ppermute | solution.py:14
  13.5 3.3 %collective-permute-start = (s32[1]{0:T(128)}, s32[1]{0:T(128)}, u32[]{:S(2)}, u32[]{:S(2)}) collective-permute-start(s32[1]{0:T(128)} %bitcast), channel_id=1, source_target_pairs={{0,16},{16,32},{32,48},{48,64},{64,80},{80,96},{96,112},{112,128},... | collective-permute-start | bytes 20 | tf_op jit(solution)/shard_map/ppermute | solution.py:14
  16.9 0.9 %broadcast_multiply_fusion = f32[46656]{0:T(1024)S(1)} fusion(f32[46656]{0:T(1024)} %param.5), kind=kLoop, calls=%fused_computation.86 | loop fusion | flops 46656 | bytes 373248 | tf_op jit(solution)/shard_map/div | solution.py:59
  17.8 0.2 mul.321
  18.0 0.1 negate_convert_fusion
  18.1 0.1 cosine_convert_fusion
  18.2 8.9 %collective-permute-done.1 = bf16[1,2,46656]{2,1,0:T(2,128)(2,1)S(1)} collective-permute-done((bf16[1,2,46656]{2,1,0:T(2,128)(2,1)}, bf16[1,2,46656]{2,1,0:T(2,128)(2,1)S(1)}, u32[]{:S(2)}, u32[]{:S(2)}) %collective-permute-start.1) | collective-permute-done | bytes 186656 | tf_op jit(solution)/shard_map/ppermute | solution.py:14
  27.1 4.2 %collective-permute-start.3 = (bf16[1,2,46656]{2,1,0:T(2,128)(2,1)S(1)}, bf16[1,2,46656]{2,1,0:T(2,128)(2,1)S(1)}, u32[]{:S(2)}, u32[]{:S(2)}) collective-permute-start(bf16[1,2,46656]{2,1,0:T(2,128)(2,1)S(1)} %collective-permute-done.1), channel_id=1, source_target_pairs={{0,1},{1,2},{2,3},{3,4},{4,5},{5,6},{6,7},{7,8},{8,9},{9,10},{10,1... | collective-permute-start | bytes 559880 | tf_op jit(solution)/shard_map/ppermute | solution.py:14
  31.3 0.1 fusion.78
  31.5 0.0 collective-permute-done
  32.2 1.9 %collective-permute-start.2 = (s32[1]{0:T(128)}, s32[1]{0:T(128)}, u32[]{:S(2)}, u32[]{:S(2)}) collective-permute-start(s32[1]{0:T(128)} %collective-permute-done), channel_id=1, source_target_pairs={{0,1},{1,2},{2,3},{3,4},{4,5},{5,6},{6,7},{7,8},{8,9},{9,10},{10,1... | collective-permute-start | bytes 20 | tf_op jit(solution)/shard_map/ppermute | solution.py:14
  34.1 1.7 %collective-permute-done.2 = s32[1]{0:T(128)} collective-permute-done((s32[1]{0:T(128)}, s32[1]{0:T(128)}, u32[]{:S(2)}, u32[]{:S(2)}) %collective-permute-start.2) | collective-permute-done | bytes 36 | tf_op jit(solution)/shard_map/ppermute | solution.py:14
  36.4 3.8 %convert_reduce_fusion.1 = (bf16[46656]{0:T(1024)(128)(2,1)S(1)}, bf16[46656]{0:T(1024)(128)(2,1)S(1)}, bf16[46656]{0:T(1024)(128)(2,1)S(1)}, bf16[46656]{0:T(1024)(128)(2,1)S(1)}) fusion(bf16[1,2,46656]{2,1,0:T(2,128)(2,1)} %bitcast.326, bf16[1,2,46656]{2,1,0:T(2,128)(2,1)S(1)} %collective-permute-done.3, bf16[1,2,46656]{2,1,0:T(2,128)(2,1)S(1)} %collective-permute-done.1), kind=kLoop, calls=%fused_computation.83 | loop fusion | flops 1026432 | bytes 933120 | tf_op jit(solution)/shard_map/convert.15
  40.1 0.2 stack.84
  40.3 0.2 stack.85
  40.5 0.3 fusion.7
  40.8 0.6 reshape.535
  41.4 0.9 %convert_bitcast_fusion.1 = f32[1,2,36,36,36]{4,3,1,2,0:T(8,128)S(1)} fusion(bf16[1,2,36,36]{3,2,1,0:T(8,128)(2,1)S(1)} %get-tuple-element.14, bf16[1,2,36,36]{3,2,1,0:T(8,128)(2,1)S(1)} %get-tuple-element.15, bf16[2,36,36,36]{3,2,1,0:T(8,128)(2,1)S(1)} %reshape.535), kind=kOutput, calls=%fused_computation.16 | convolution fusion | flops 27195264 | bytes 570240 | tf_op jit(solution)/shard_map/uavb,pvxyb->puxya/dot_general | solution.py:34
  42.3 1.1 %reshape.496 = f32[2,36,1296]{2,0,1:T(2,128)S(1)} reshape(f32[1,2,36,36,36]{4,3,1,2,0:T(8,128)S(1)} %convert_bitcast_fusion.1) | data formatting | bytes 746496 | tf_op jit(solution)/shard_map/convert_element_type | solution.py:59
  43.3 0.2 stack.97
  43.5 0.2 stack.98
  43.7 0.3 fusion.5
  44.0 0.6 reshape.537
  44.6 0.9 %convert_bitcast_fusion = f32[1,2,36,36,36]{4,3,1,2,0:T(8,128)S(1)} fusion(bf16[1,2,36,36]{3,2,1,0:T(8,128)(2,1)S(1)} %get-tuple-element.14, bf16[1,2,36,36]{3,2,1,0:T(8,128)(2,1)S(1)} %get-tuple-element.15, bf16[2,36,36,36]{3,2,1,0:T(8,128)(2,1)S(1)} %reshape.537), kind=kOutput, calls=%fused_computation.15 | convolution fusion | flops 27195264 | bytes 570240 | tf_op jit(solution)/shard_map/uavb,pvxyb->puxya/dot_general | solution.py:34
  45.5 1.1 %reshape.497 = f32[2,36,1296]{2,0,1:T(2,128)S(1)} reshape(f32[1,2,36,36,36]{4,3,1,2,0:T(8,128)S(1)} %convert_bitcast_fusion) | data formatting | bytes 746496 | tf_op jit(solution)/shard_map/convert_element_type | solution.py:59
  46.5 1.0 %multiply_convert_fusion = (bf16[2,36,1296]{2,0,1:T(2,128)(2,1)S(1)}, bf16[2,36,1296]{2,0,1:T(2,128)(2,1)}) fusion(f32[2,36,1296]{2,0,1:T(2,128)S(1)} %reshape.497, f32[36,1296]{1,0:T(8,128)S(1)} %mul.321, f32[2,36,1296]{2,0,1:T(2,128)S(1)} %reshape.496), kind=kLoop, calls=%fused_computation.47 | loop fusion | flops 373248 | bytes 1306368 | tf_op jit(solution)/shard_map/convert_element_type | solution.py:59
  47.6 0.3 fusion.4
  47.8 0.6 reshape.538
  48.5 0.9 %convolution_bitcast_fusion.4 = f32[1,2,36,36,36]{4,3,1,2,0:T(8,128)S(1)} fusion(bf16[1,2,36,36]{3,2,1,0:T(8,128)(2,1)S(1)} %get-tuple-element.13, bf16[1,2,36,36]{3,2,1,0:T(8,128)(2,1)S(1)} %get-tuple-element.12, bf16[2,36,36,36]{3,2,1,0:T(8,128)(2,1)S(1)} %reshape.538), kind=kOutput, calls=%fused_computation.23 | convolution fusion | flops 27008640 | bytes 570240 | tf_op jit(solution)/shard_map/uavb,pvxyb->puxya/dot_general | solution.py:34
  49.3 0.1 copy.47
  49.5 1.7 %reshape_reshape.9 = f32[1,1,2,46656]{3,2,1,0:T(2,128)} reshape(f32[1,2,36,36,36]{4,3,2,1,0:T(8,128)S(1)} %copy.47) | data formatting | bytes 746496 | tf_op jit(solution)/shard_map/reshape;reshape | solution.py:61
  51.2 0.3 fusion.6
  51.5 0.8 %reshape.536 = bf16[2,36,36,36]{3,2,1,0:T(8,128)(2,1)S(1)} reshape(bf16[1,2,36,1296]{3,2,1,0:T(8,128)(2,1)S(1)} %fusion.6) | data formatting | bytes 373248 | tf_op jit(solution)/shard_map/reshape.20
  52.3 0.9 %convolution_bitcast_fusion.5 = f32[1,2,36,36,36]{4,3,1,2,0:T(8,128)S(1)} fusion(bf16[1,2,36,36]{3,2,1,0:T(8,128)(2,1)S(1)} %get-tuple-element.13, bf16[1,2,36,36]{3,2,1,0:T(8,128)(2,1)S(1)} %get-tuple-element.12, bf16[2,36,36,36]{3,2,1,0:T(8,128)(2,1)S(1)} %reshape.536), kind=kOutput, calls=%fused_computation.24 | convolution fusion | flops 27008640 | bytes 570240 | tf_op jit(solution)/shard_map/uavb,pvxyb->puxya/dot_general | solution.py:34
  53.1 0.1 copy.39
  53.3 1.0 %reshape_reshape.8 = f32[1,1,2,46656]{3,2,1,0:T(2,128)S(1)} reshape(f32[1,2,36,36,36]{4,3,2,1,0:T(8,128)S(1)} %copy.39) | data formatting | bytes 746496 | tf_op jit(solution)/shard_map/reshape;reshape | solution.py:61
  54.2 0.0 copy-done
  54.2 1.5 %multiply_add_fusion.1 = (bf16[1,1,46656]{2,1,0:T(2,128)(2,1)S(1)}, bf16[1,1,46656]{2,1,0:T(2,128)(2,1)S(1)}) fusion(f32[1,1,2,46656]{3,2,1,0:T(2,128)S(1)} %reshape_reshape.8, f32[1,1,2,46656]{3,2,1,0:T(2,128)S(1)} %copy-done, f32[]{:T(128)} %bitcast.45, f32[]{:T(128)} %bitcast.1, bf16[1,2,46656]{2,1,0:T(2,128)(2,1)S(1)} %collective-permute-done.1, ...), kind=kLoop, calls=%fused_computation.81 | loop fusion | flops 1119744 | bytes 1306376 | tf_op jit(solution)/shard_map/add | solution.py:65
  55.7 1.1 %pad_maximum_fusion = bf16[1,1,2,46656]{3,2,1,0:T(2,128)(2,1)} fusion(bf16[1,1,1,46656]{3,2,1,0:T(2,128)(2,1)S(1)} %bitcast.327, bf16[1,1,1,46656]{3,2,1,0:T(2,128)(2,1)S(1)} %bitcast.328), kind=kLoop, calls=%fused_computation.69 | loop fusion | flops 373248 | bytes 373248 | tf_op jit(solution)/shard_map/stack | solution.py:112
  56.8 2.9 %all-gather.3.cloned.1.call-done = bf16[16,1,2,46656]{3,2,1,0:T(2,128)(2,1)} async-done(((bf16[1,1,2,46656]{3,2,1,0:T(2,128)(2,1)}), bf16[16,1,2,46656]{3,2,1,0:T(2,128)(2,1)}) %all-gather.3.cloned.1.call-update) | async-done | bytes 2986000 | tf_op jit(solution)/shard_map/all_gather | solution.py:115
  59.7 2.1 %copy.118 = bf16[16,1,2,46656]{3,0,2,1:T(8,128)(2,1)S(1)} copy(bf16[16,1,2,46656]{3,2,1,0:T(2,128)(2,1)} %all-gather.3.cloned.1.call-done) | data formatting | bytes 5971968 | tf_op jit(solution)/shard_map/all_gather | solution.py:115
  61.8 0.5 fusion.18
  62.3 0.6 fusion.19
  62.9 0.5 fusion.25
  63.4 0.5 fusion.23
  64.0 0.6 maximum_multiply_fusion
  (5 shorter events, 0.0 us)
Async XLA Ops:
  7.2 52.5 %all-gather.3.cloned.1.call-start = ((), (), s32[]{:S(2)}) async-start(), calls=%async_computation | async-start | bytes 3176960 | tf_op jit(solution)/shard_map/all_gather | solution.py:115
  7.9 19.2 %collective-permute-start.1 = (bf16[1,2,46656]{2,1,0:T(2,128)(2,1)}, bf16[1,2,46656]{2,1,0:T(2,128)(2,1)S(1)}, u32[]{:S(2)}, u32[]{:S(2)}) collective-permute-start(bf16[1,2,46656]{2,1,0:T(2,128)(2,1)} %bitcast.325), channel_id=1, source_target_pairs={{0,16},{16,32},{32,48},{48,64},{64,80},{80,96},{96,112},{112,128},... | collective-permute-start | bytes 559880 | tf_op jit(solution)/shard_map/ppermute | solution.py:14
  13.5 17.9 %collective-permute-start = (s32[1]{0:T(128)}, s32[1]{0:T(128)}, u32[]{:S(2)}, u32[]{:S(2)}) collective-permute-start(s32[1]{0:T(128)} %bitcast), channel_id=1, source_target_pairs={{0,16},{16,32},{32,48},{48,64},{64,80},{80,96},{96,112},{112,128},... | collective-permute-start | bytes 20 | tf_op jit(solution)/shard_map/ppermute | solution.py:14
  27.1 9.3 %collective-permute-start.3 = (bf16[1,2,46656]{2,1,0:T(2,128)(2,1)S(1)}, bf16[1,2,46656]{2,1,0:T(2,128)(2,1)S(1)}, u32[]{:S(2)}, u32[]{:S(2)}) collective-permute-start(bf16[1,2,46656]{2,1,0:T(2,128)(2,1)S(1)} %collective-permute-done.1), channel_id=1, source_target_pairs={{0,1},{1,2},{2,3},{3,4},{4,5},{5,6},{6,7},{7,8},{8,9},{9,10},{10,1... | collective-permute-start | bytes 559880 | tf_op jit(solution)/shard_map/ppermute | solution.py:14
  32.2 3.6 %collective-permute-start.2 = (s32[1]{0:T(128)}, s32[1]{0:T(128)}, u32[]{:S(2)}, u32[]{:S(2)}) collective-permute-start(s32[1]{0:T(128)} %collective-permute-done), channel_id=1, source_target_pairs={{0,1},{1,2},{2,3},{3,4},{4,5},{5,6},{6,7},{7,8},{8,9},{9,10},{10,1... | collective-permute-start | bytes 20 | tf_op jit(solution)/shard_map/ppermute | solution.py:14
  49.4 1.7 %copy-start.1 = (bf16[2,36,1296]{2,0,1:T(2,128)(2,1)S(1)}, bf16[2,36,1296]{2,0,1:T(2,128)(2,1)}, u32[]{:S(2)}) copy-start(bf16[2,36,1296]{2,0,1:T(2,128)(2,1)} %get-tuple-element.11) | copy-start | bytes 559876
  53.2 1.0 %copy-start = (f32[1,1,2,46656]{3,2,1,0:T(2,128)S(1)}, f32[1,1,2,46656]{3,2,1,0:T(2,128)}, u32[]{:S(2)}) copy-start(f32[1,1,2,46656]{3,2,1,0:T(2,128)} %reshape_reshape.9) | copy-start | bytes 1119748
Sparse Core Ops, SparseCore 0:
  10.1 49.5 all-gather.2
where the time goes:
time: 71.7 us; the launch traced here: 71.4 us
  between operations  15.5 us (22%)
  starting transfers between devices  15.2 us (21%)
  waiting for transfers between devices  14.1 us (20%)
  local copies, waits for them, and re-layouts  10.6 us (15%)
  other arithmetic  9.25 us (13%)
  matrix products  6.74 us (9%)
    ppermute x4, starting transfers between devices, shifted(): lax.ppermute(array, axis, [(i, (i + by) % length) for i in range(length)])  15.1 us
    ppermute x4, waiting for transfers between devices, shifted(): lax.ppermute(array, axis, [(i, (i + by) % length) for i in range(length)])  10.5 us
    another operation x4, other arithmetic  4.09 us
    dot_general x4, matrix products, transform(): jnp.einsum('uavb,pvxyb->puxya', matrix, current, preferred_element_type=j...  3.56 us
    all_gather x1, waiting for transfers between devices, shards(): lax.all_gather(local_bands, 'band', axis=0, tiled=True)  2.86 us
    another operation x2, local copies, waits for them, and re-layouts, add_block(): potential = potential.reshape(visits, owned, 2, potential.shape[2])  2.7 us
    another operation x4, local copies, waits for them, and re-layouts  2.63 us
    dot_general x4, matrix products, contract(): return jnp.einsum('ig,jg->ij', x, y, preferred_element_type=jnp.float32)  2.14 us
  transfers between devices with their start and end apart: 5, of which 3 were waited for; matrix products, arithmetic and copies ran while one was open for 30% of the time, Pallas kernels for 0%

commit v1 on v0

v1 whole, which is shorter than its diff:
```python
import functools
import math

import jax
import jax.numpy as jnp
import numpy as np
from jax import lax
from jax.experimental import pallas as pl
from jax.experimental.pallas import tpu as pltpu
from jax.sharding import PartitionSpec as P

NG = 36
GRID = 46656
SIDE = 216
NX = 4
F32 = jnp.float32
BF16 = jnp.bfloat16


def tables():
    index = np.arange(SIDE)
    x, y_high = index // 6, index % 6
    rows = (np.outer(x, x) + 6 * np.outer(y_high, y_high)) % NG
    y_low, z = index // NG, index % NG
    lanes = (np.outer(z, z) + 6 * np.outer(y_low, y_low)) % NG
    twiddle = np.outer(y_high, y_low) % NG
    step = 2.0 * math.pi / NG
    mats = np.stack([np.cos(step * rows), np.sin(step * rows), np.cos(step * lanes), np.sin(step * lanes)])
    turns = np.stack([np.cos(step * twiddle), np.sin(step * twiddle)])
    return jnp.asarray(mats.astype(np.float32)).astype(BF16), jnp.asarray(turns.astype(np.float32))


def dot(a, b):
    return jnp.dot(a, b, preferred_element_type=F32)


def exchange_pair(own, other, weight, mats, twiddle, kernel):
    c, d = own[0].astype(F32), own[1].astype(F32)
    a, b = other[0].astype(F32), other[1].astype(F32)
    re, im = (a * c + b * d).astype(BF16), (a * d - b * c).astype(BF16)
    cos, sin = mats[0], mats[1]
    turn_re, turn_im = twiddle[0], twiddle[1]
    u, v = dot(cos, re) + dot(sin, im), dot(cos, im) - dot(sin, re)
    re, im = (u * turn_re + v * turn_im).astype(BF16), (v * turn_re - u * turn_im).astype(BF16)
    cos, sin = mats[2], mats[3]
    scale = kernel[...]
    u, v = dot(re, cos) + dot(im, sin), dot(im, cos) - dot(re, sin)
    re, im = (u * scale).astype(BF16), (v * scale).astype(BF16)
    u, v = dot(re, cos) - dot(im, sin), dot(im, cos) + dot(re, sin)
    re, im = (u * turn_re - v * turn_im).astype(BF16), (v * turn_re + u * turn_im).astype(BF16)
    cos, sin = mats[0], mats[1]
    e, f = dot(cos, re) - dot(sin, im), dot(cos, im) + dot(sin, re)
    return weight * (a * e - b * f), weight * (a * f + b * e)


def kernel_body(
    n_pool, own, occ, kernel, mats, twiddle, out, gram,
    first, second, occ1, occ2, slots, accum, partial,
    pool_send, pool_recv, next_send, next_recv, slot_recv, ring_send, mate_send,
):
    k, band = lax.axis_index("pool"), lax.axis_index("band")
    n_band = 4 * NX
    y, x, core = band // (2 * NX), (band // 2) % NX, band % 2

    def at(yy, xx, cc):
        return yy * (2 * NX) + xx * 2 + cc

    here = k
    ahead, behind = (k + 1) % n_pool, (k + n_pool - 1) % n_pool
    right, left = (x + 1) % NX, (x + NX - 1) % NX
    x_up, x_down = at(y, right, core), at(y, left, core)
    y_mate, mate = at(1 - y, x, core), at(y, x, 1 - core)
    band_up, band_down = (band + 1) % n_band, (band + n_band - 1) % n_band

    barrier = pltpu.get_barrier_semaphore()
    greeted = [(ahead, band), (behind, band)]
    greeted += [(here, b) for b in (band_up, band_down, x_up, x_down, y_mate, mate)]
    for device in greeted:
        pl.semaphore_signal(barrier, inc=1, device_id=device, device_id_type=pl.DeviceIdType.MESH)
    pl.semaphore_wait(barrier, len(greeted))

    started = []

    def send(src, dst, send_sem, recv_sem, device):
        copy = pltpu.make_async_remote_copy(
            src_ref=src, dst_ref=dst, send_sem=send_sem, recv_sem=recv_sem,
            device_id=device, device_id_type=pl.DeviceIdType.MESH,
        )
        copy.start()
        started.append(copy)

    def arrive(dst, recv_sem, send_sem):
        pltpu.make_async_remote_copy(
            src_ref=dst, dst_ref=dst, send_sem=send_sem, recv_sem=recv_sem,
            device_id=(here, band), device_id_type=pl.DeviceIdType.MESH,
        ).wait_recv()

    counts = {"ring": 0, "mate": 0}

    def pass_on(kind, src, slot, part, to):
        sems = ring_send if kind == "ring" else mate_send
        send(src, slots.at[slot, part], sems.at[counts[kind]], slot_recv.at[slot, part], (here, to))
        counts[kind] += 1

    def take(slot, part):
        arrive(slots.at[slot, part], slot_recv.at[slot, part], ring_send.at[0])

    send(occ, occ1, pool_send.at[2], pool_recv.at[2], (ahead, band))
    for part in range(2):
        send(own.at[part], first.at[part], pool_send.at[part], pool_recv.at[part], (ahead, band))
    for part in range(2):
        for to in (x_up, x_down):
            pass_on("ring", own.at[part], band, part, to)
    for part in range(2):
        pass_on("ring", own.at[part], band, part, y_mate)
    for part in range(2):
        pass_on("mate", own.at[part], band, part, mate)

    def relay(slot, part, to):
        take(slot, part)
        for target in to:
            pass_on("mate" if target is mate else "ring", slots.at[slot, part], slot, part, target)

    relay(x_down, 0, (x_up, mate))
    relay(x_up, 1, (x_down, mate))
    relay(x_down, 1, (mate,))
    relay(x_up, 0, (mate,))

    arrive(occ1, pool_recv.at[2], pool_send.at[2])
    send(occ1, occ2, next_send.at[2], next_recv.at[2], (here, band_up))
    for part in range(2):
        arrive(first.at[part], pool_recv.at[part], pool_send.at[part])
        send(first.at[part], second.at[part], next_send.at[part], next_recv.at[part], (here, band_up))

    weight = -0.5 * occ1[...].astype(F32)
    re, im = exchange_pair(own, first, weight, mats, twiddle, kernel)
    accum[0], accum[1] = re, im

    relay(y_mate, 0, (x_up, x_down, mate))
    relay(y_mate, 1, (x_up, x_down, mate))

    arrive(occ2, next_recv.at[2], next_send.at[2])
    for part in range(2):
        arrive(second.at[part], next_recv.at[part], next_send.at[part])
    weight = -0.5 * occ2[...].astype(F32)
    re, im = exchange_pair(own, second, weight, mats, twiddle, kernel)
    re, im = (accum[0] + re).astype(BF16), (accum[1] + im).astype(BF16)
    out[0], out[1] = re, im
    accum[0], accum[1] = re.astype(F32), im.astype(F32)

    other_down, other_up = at(1 - y, left, core), at(1 - y, right, core)
    far, other_far = at(y, (x + 2) % NX, core), at(1 - y, (x + 2) % NX, core)
    relay(other_down, 0, (x_up, mate))
    relay(other_up, 1, (x_down, mate))
    relay(other_down, 1, (mate,))
    relay(other_up, 0, (mate,))
    relay(far, 0, (mate,))
    relay(far, 1, (mate,))

    def overlap(ref, slot):
        c, d = ref[0].astype(F32), ref[1].astype(F32)
        e, f = accum[0], accum[1]
        partial[slot] = (c * e + d * f).reshape(SIDE // 8, 8, SIDE).sum(0)
        partial[slot + n_band] = (c * f - d * e).reshape(SIDE // 8, 8, SIDE).sum(0)

    overlap(own, band)
    for slot in (x_down, x_up, y_mate, other_down, other_up, far):
        overlap(slots.at[slot], slot)
    relay(other_far, 0, (mate,))
    relay(other_far, 1, (mate,))
    overlap(slots.at[other_far], other_far)
    twin = 1 - core
    order = [(y, x), (y, left), (y, right), (1 - y, x), (1 - y, left), (1 - y, right)]
    order += [(y, (x + 2) % NX), (1 - y, (x + 2) % NX)]
    for yy, xx in order:
        slot = at(yy, xx, twin)
        take(slot, 0)
        take(slot, 1)
        overlap(slots.at[slot], slot)

    sums = partial[...].sum(axis=1)
    ones = jnp.full((8, SIDE), 1.0 / math.sqrt(GRID), F32)
    line = lax.dot_general(
        ones, sums, (((1,), (1,)), ((), ())), precision=lax.Precision.HIGHEST, preferred_element_type=F32
    )
    gram[0] = line[0:1, 0:n_band]
    gram[1] = line[0:1, n_band : 2 * n_band]

    for copy in started:
        copy.wait_send()


def shards(n_pool, orbitals, occupation, kernel):
    n_band = 4 * NX
    own = orbitals.reshape(2, SIDE, SIDE)
    scale = (kernel / GRID).reshape(NG, 6, 6, NG).transpose(0, 2, 1, 3).reshape(SIDE, SIDE)
    mats, twiddle = tables()
    vmem = pl.BlockSpec(memory_space=pltpu.VMEM)
    pair = pltpu.VMEM((2, SIDE, SIDE), BF16)
    dma = pltpu.SemaphoreType.DMA
    exchanged, gram = pl.pallas_call(
        functools.partial(kernel_body, n_pool),
        out_shape=(
            jax.ShapeDtypeStruct((2, SIDE, SIDE), BF16),
            jax.ShapeDtypeStruct((2, 1, n_band), F32),
        ),
        in_specs=[vmem, vmem, vmem, vmem, vmem],
        out_specs=(vmem, vmem),
        scratch_shapes=[
            pair, pair, pltpu.VMEM((1, 1), jnp.int32), pltpu.VMEM((1, 1), jnp.int32),
            pltpu.VMEM((n_band, 2, SIDE, SIDE), BF16),
            pltpu.VMEM((2, SIDE, SIDE), F32),
            pltpu.VMEM((2 * n_band, 8, SIDE), F32),
            dma((3,)), dma((3,)), dma((3,)), dma((3,)), dma((n_band, 2)), dma((14,)), dma((16,)),
        ],
        compiler_params=pltpu.CompilerParams(
            collective_id=0, has_side_effects=True, vmem_limit_bytes=50 * 1024 * 1024
        ),
    )(own, occupation, scale, mats, twiddle)
    return exchanged.reshape(1, 1, 2, GRID), gram.reshape(1, 2, n_band, 1)


def solution(mesh):
    return jax.shard_map(
        functools.partial(shards, mesh.shape["pool"]),
        mesh=mesh,
        in_specs=(P("pool", "band", None, None), P("pool", "band"), P()),
        out_specs=(P("pool", "band", None, None), P("pool", None, None, "band")),
        check_vma=False,
    )
```

time: 71.7 us -> 42.7 us (0.60)
  Pallas kernels: 0 us -> 36.2 us
  starting transfers between devices: 15.2 us -> 0 us
  between operations: 15.5 us -> 1.36 us
  waiting for transfers between devices: 14.1 us -> 0 us
  other arithmetic: 9.25 us -> 0.94 us
  matrix products: 6.74 us -> 0 us
  local copies, waits for them, and re-layouts: 10.6 us -> 3.96 us
    pallas_call x0 -> x1, Pallas kernels: none -> 36.2 us  [shards(): pl.pallas_call(functools.partial(kernel_body, n_pool), out_shape=(jax.Sha...]
    ppermute x4 -> x0, starting transfers between devices: 15.1 us -> none  [shifted(): lax.ppermute(array, axis, [(i, (i + by) % length) for i in range(length)])]
    ppermute x4 -> x0, waiting for transfers between devices: 10.5 us -> none  [shifted(): lax.ppermute(array, axis, [(i, (i + by) % length) for i in range(length)])]
    dot_general x12 -> x0, matrix products: 6.74 us -> none  [the longest x4 3.56 us: transform(): jnp.einsum('uavb,pvxyb->puxya', matrix, current, preferred_element_type=j...]
    another operation x10 -> x0, local copies, waits for them, and re-layouts: 6.04 us -> none  [the longest x2 2.7 us: add_block(): potential = potential.reshape(visits, owned, 2, potential.shape[2])]
    another operation x6 -> x0, other arithmetic: 5.21 us -> none
    all_gather x1 -> x0, waiting for transfers between devices: 2.86 us -> none  [shards(): lax.all_gather(local_bands, 'band', axis=0, tiled=True)]
    reshape x0 -> x4, local copies, waits for them, and re-layouts: none -> 2.53 us  [the longest x1 1.23 us: shards(): return (exchanged.reshape(1, 1, 2, GRID), gram.reshape(1, 2, n_band, 1))]
  transfers between devices with their start and end apart: 5 -> 0, of which waited for: 3 -> 0; matrix products, arithmetic and copies ran while one was open for 30% -> 0% of each run, Pallas kernels for 0% -> 0%
where the time goes in v1:
time: 42.7 us; the launch traced here: 42.5 us
  Pallas kernels  36.2 us (85%)
  local copies, waits for them, and re-layouts  3.96 us (9%)
  between operations  1.36 us (3%)
  other arithmetic  0.94 us (2%)
    pallas_call x1, Pallas kernels, shards(): pl.pallas_call(functools.partial(kernel_body, n_pool), out_shape=(jax.Sha...  36.2 us
    unnamed x7, local copies, waits for them, and re-layouts  1.25 us
    reshape x1, local copies, waits for them, and re-layouts, shards(): return (exchanged.reshape(1, 1, 2, GRID), gram.reshape(1, 2, n_band, 1))  1.23 us
    div x1, other arithmetic, shards(): kernel / GRID  0.94 us

profile of v1, /device:TPU:1, one launch (start us, length us, event | category | flops | bytes accessed | tf_op | source)
XLA Modules:
  0.0 42.5 jit_solution(2518153051878783504)
XLA Ops:
  0.6 0.9 %broadcast_multiply_fusion = f32[46656]{0:T(1024)S(1)} fusion(f32[46656]{0:T(1024)} %param.7), kind=kLoop, calls=%fused_computation | loop fusion | flops 46656 | bytes 373248 | tf_op jit(solution)/shard_map/div | solution.py:196
  1.6 0.5 %reshape.20 = f32[36,6,6,36]{3,2,1,0:T(8,128)S(1)} reshape(f32[46656]{0:T(1024)S(1)} %broadcast_multiply_fusion) | data formatting | bytes 373248 | tf_op jit(solution)/shard_map/reshape | solution.py:196
  2.1 0.2 copy.8
  2.2 0.0 copy-start.2
  2.3 0.0 copy-start
  2.3 0.0 copy-start.1
  2.3 0.2 reshape.21.kernel
  2.5 0.7 %copy-done.2 = bf16[1,1,2,46656]{3,2,1,0:T(2,128)(2,1)S(1)} copy-done((bf16[1,1,2,46656]{3,2,1,0:T(2,128)(2,1)S(1)}, bf16[1,1,2,46656]{3,2,1,0:T(2,128)(2,1)}, u32[]{:S(2)}) %copy-start.2) | copy-done | bytes 186648
  3.2 0.6 %reshape.19.own = bf16[2,216,216]{2,1,0:T(8,128)(2,1)S(1)} reshape(bf16[1,1,2,46656]{3,2,1,0:T(2,128)(2,1)S(1)} %copy-done.2) | data formatting | bytes 373248 | tf_op jit(solution)/shard_map/reshape | solution.py:195
  4.4 0.0 copy-done
  4.5 0.0 copy-done.1
  4.5 36.2 %shard_map.68 = (bf16[2,216,216]{2,1,0:T(8,128)(2,1)S(1)}, f32[2,1,16]{2,1,0:T(1,128)S(1)}) custom-call(bf16[2,216,216]{2,1,0:T(8,128)(2,1)S(1)} %reshape.19.own, s32[1,1]{1,0:T(1,128)S(6)} %copy.11.occ, f32[216,216]{1,0:T(8,128)S(1)} %reshape.21.kernel, bf16[4,216,216]{2,1,0:T(8,128)(2,1)S(1)} %copy-done, f32[2,216,216]{2,1,0:T(8,128)S(1)} %copy-done.1), custom_call_target="tpu_custom_call" | custom-call | tf_op jit(solution)/shard_map/pallas_call | solution.py:201
  40.7 1.2 %reshape.22 = bf16[1,1,2,46656]{3,2,1,0:T(2,128)(2,1)} reshape(bf16[2,216,216]{2,1,0:T(8,128)(2,1)S(1)} %get-tuple-element.4) | data formatting | bytes 373248 | tf_op jit(solution)/shard_map/reshape | solution.py:220
  41.9 0.6 %copy.12 = f32[1,2,16,1]{2,3,1,0:T(1,128)} copy(f32[1,2,16,1]{2,3,1,0:T(1,128)S(1)} %bitcast.4) | data formatting | bytes 256
Async XLA Ops:
  2.2 0.9 %copy-start.2 = (bf16[1,1,2,46656]{3,2,1,0:T(2,128)(2,1)S(1)}, bf16[1,1,2,46656]{3,2,1,0:T(2,128)(2,1)}, u32[]{:S(2)}) copy-start(bf16[1,1,2,46656]{3,2,1,0:T(2,128)(2,1)} %param.5) | copy-start | bytes 559876
  2.3 2.2 %copy-start = (bf16[4,216,216]{2,1,0:T(8,128)(2,1)S(1)}, bf16[4,216,216]{2,1,0:T(8,128)(2,1)}, u32[]{:S(2)}) copy-start(bf16[4,216,216]{2,1,0:T(8,128)(2,1)} %constant.11.mats) | copy-start | bytes 1119748
  2.3 2.2 %copy-start.1 = (f32[2,216,216]{2,1,0:T(8,128)S(1)}, f32[2,216,216]{2,1,0:T(8,128)}, u32[]{:S(2)}) copy-start(f32[2,216,216]{2,1,0:T(8,128)} %constant.8.clone.twiddle) | copy-start | bytes 1119748

commit v2 on v1

v2 whole, which is shorter than its diff:
```python
import functools
import math

import jax
import jax.numpy as jnp
import numpy as np
from jax import lax
from jax.experimental import pallas as pl
from jax.experimental.pallas import tpu as pltpu
from jax.sharding import PartitionSpec as P

NG = 36
GRID = 46656
SIDE = 216
WIDE = 256
DENSE = 368
BLOCK = 1024
FULL = GRID // BLOCK
TAIL = GRID - FULL * BLOCK
NX = 4
F32 = jnp.float32
BF16 = jnp.bfloat16
HALVES = ((0, 23296), (23296, 23360))
QUARTERS = ((0, 11648), (11648, 11648), (23296, 11648), (34944, 11712))


def tables():
    index = np.arange(SIDE)
    x, y_high = index // 6, index % 6
    rows = (np.outer(x, x) + 6 * np.outer(y_high, y_high)) % NG
    y_low, z = index // NG, index % NG
    lanes = (np.outer(z, z) + 6 * np.outer(y_low, y_low)) % NG
    twiddle = np.outer(y_high, y_low) % NG
    step = 2.0 * math.pi / NG

    def both(phases, shape):
        out = np.zeros((2,) + shape, np.float32)
        out[:, :SIDE, :SIDE] = np.stack([np.cos(step * phases), np.sin(step * phases)])
        return jnp.asarray(out)

    return (
        both(rows, (SIDE, SIDE)).astype(BF16),
        both(lanes, (WIDE, WIDE)).astype(BF16),
        both(twiddle, (SIDE, WIDE)),
    )


def dot(a, b):
    return jnp.dot(a, b, preferred_element_type=F32)


def lane_index(rows):
    return lax.broadcasted_iota(jnp.int32, (rows, 128), 1)


def unpack(raw, dense):
    for t in range(FULL):
        dense[:, pl.ds(8 * t, 8), :] = raw[:, pl.ds(BLOCK * t, BLOCK)].astype(F32).reshape(2, 8, 128)
    for j in range(0, TAIL, 128):
        width = min(128, TAIL - j)
        dense[:, 8 * FULL + j // 128, 0:width] = raw[:, pl.ds(FULL * BLOCK + j, width)].astype(F32)


def to_planes(dense, planes):
    for start in range(16):
        count = 14 if start < 8 else 13
        row, shift = (SIDE * start) // 128, (SIDE * start) % 128
        low = dense[pl.ds(row, count, stride=27), :]
        high = dense[pl.ds(row + 1, count, stride=27), :]
        if shift:
            low, high = pltpu.roll(low, 128 - shift, 1), pltpu.roll(high, 128 - shift, 1)
            keep = lane_index(count) < 128 - shift
            low = jnp.where(keep, low, high)
            if shift + SIDE > 256:
                last = pltpu.roll(dense[pl.ds(row + 2, count, stride=27), :], 128 - shift, 1)
                high = jnp.where(keep, high, last)
        planes[0, pl.ds(start, count, stride=16), :] = low
        planes[1, pl.ds(start, count, stride=16), :] = high


def to_dense(planes, dense):
    for q in range(27):
        count = 14 if q <= 12 else 13
        total, lane = None, lane_index(count)
        pos = 0
        while pos < 128:
            row, col = divmod(128 * q + pos, SIDE)
            plane, first = (0, 0) if col < 128 else (1, 128)
            width = min((SIDE if plane else 128) - col, 128 - pos)
            piece = planes[plane, pl.ds(row, count, stride=16), :]
            shift = (pos - (col - first)) % 128
            if shift:
                piece = pltpu.roll(piece, shift, 1)
            total = piece if total is None else jnp.where(lane < pos, total, piece)
            pos += width
        dense[pl.ds(q, count, stride=27), :] = total
    row, col = divmod(364 * 128, SIDE)
    dense[364:365, 0:64] = planes[1, row : row + 1, col - 128 : col - 64]


def permute_scale(planes, scale):
    lane = lane_index(NG)
    for low in range(6):
        for plane in range(2):
            total = jnp.zeros((NG, 128), F32)
            for high in range(6):
                pos, end = max(NG * high, 128 * plane), min(NG * high + NG, 128 * plane + 128)
                while pos < end:
                    col = NG * low + pos - NG * high
                    source = col // 128
                    width = min(end - pos, 128 * (source + 1) - col)
                    piece = planes[source, pl.ds(high, NG, stride=6), :]
                    shift = (pos - col) % 128
                    if shift:
                        piece = pltpu.roll(piece, shift, 1)
                    at = pos - 128 * plane
                    total = jnp.where((lane >= at) & (lane < at + width), piece, total)
                    pos += width
            scale[plane, pl.ds(low, NG, stride=6), :] = total * (1.0 / GRID)


def wide(planes):
    return jnp.concatenate([planes[0], planes[1]], axis=1)


def exchange_pair(own, other, weight, rows, lanes, twiddle, scale):
    c, d, a, b = wide(own.at[0]), wide(own.at[1]), wide(other.at[0]), wide(other.at[1])
    re, im = (a * c + b * d).astype(BF16), (a * d - b * c).astype(BF16)
    cos, sin = rows[0], rows[1]
    turn_re, turn_im = twiddle[0], twiddle[1]
    u, v = dot(cos, re) + dot(sin, im), dot(cos, im) - dot(sin, re)
    re, im = (u * turn_re + v * turn_im).astype(BF16), (v * turn_re - u * turn_im).astype(BF16)
    cos, sin = lanes[0], lanes[1]
    factor = wide(scale)
    u, v = dot(re, cos) + dot(im, sin), dot(im, cos) - dot(re, sin)
    re, im = (u * factor).astype(BF16), (v * factor).astype(BF16)
    u, v = dot(re, cos) - dot(im, sin), dot(im, cos) + dot(re, sin)
    re, im = (u * turn_re - v * turn_im).astype(BF16), (v * turn_re + u * turn_im).astype(BF16)
    cos, sin = rows[0], rows[1]
    e, f = dot(cos, re) - dot(sin, im), dot(cos, im) + dot(sin, re)
    return weight * (a * e - b * f), weight * (a * f + b * e)


def kernel_body(
    n_pool, own, occ, kernel, rows_in, lanes_in, twiddle_in, out, gram,
    first, second, occ1, occ2, slots, flat, rows, lanes, twiddle,
    dense, own_planes, planes, accum, scale, ket, ket_turned, partial,
    local_sem, pool_send, pool_recv, next_send, next_recv, slot_recv, ring_send, mate_send,
):
    k, band = lax.axis_index("pool"), lax.axis_index("band")
    n_band = 4 * NX
    y, x, core = band // (2 * NX), (band // 2) % NX, band % 2

    def at(yy, xx, cc):
        return yy * (2 * NX) + xx * 2 + cc

    ahead, behind = (k + 1) % n_pool, (k + n_pool - 1) % n_pool
    right, left, across = (x + 1) % NX, (x + NX - 1) % NX, (x + 2) % NX
    x_up, x_down = at(y, right, core), at(y, left, core)
    y_mate, mate = at(1 - y, x, core), at(y, x, 1 - core)
    band_up, band_down = (band + 1) % n_band, (band + n_band - 1) % n_band
    mesh_id = pl.DeviceIdType.MESH

    barrier = pltpu.get_barrier_semaphore()
    senders = [(behind, band)] + [(k, b) for b in (band_down, x_up, x_down, y_mate, mate)]
    for device in senders:
        pl.semaphore_signal(barrier, inc=1, device_id=device, device_id_type=mesh_id)

    local = [
        pltpu.make_async_copy(src, dst, local_sem.at[i])
        for i, (src, dst) in enumerate(
            [(own, slots.at[band]), (kernel, flat), (rows_in, rows), (lanes_in, lanes), (twiddle_in, twiddle)]
        )
    ]
    for copy in local:
        copy.start()
    pl.semaphore_wait(barrier, len(senders))

    def remote(src, dst, send_sem, recv_sem, device):
        return pltpu.make_async_remote_copy(
            src_ref=src, dst_ref=dst, send_sem=send_sem, recv_sem=recv_sem, device_id=device, device_id_type=mesh_id
        )

    def piece(ref, span):
        return ref.at[:, pl.ds(span[0], span[1])]

    def ring(index, src, slot, part, to):
        span = HALVES[part]
        return remote(
            piece(src, span), piece(slots.at[slot], span), ring_send.at[index], slot_recv.at[slot, part], (k, to)
        )

    def to_mate(index, src, slot, part):
        span = HALVES[part]
        return remote(
            piece(src, span), piece(slots.at[slot], span), mate_send.at[index], slot_recv.at[slot, part], (k, mate)
        )

    def take(slot, part):
        ring(0, slots.at[slot], slot, part, band).wait_recv()

    other_down, other_up = at(1 - y, left, core), at(1 - y, right, core)
    far, other_far = at(y, across, core), at(1 - y, across, core)

    pool = [remote(occ, occ1, pool_send.at[4], pool_recv.at[4], (ahead, band))]
    pool += [
        remote(piece(own, span), piece(first, span), pool_send.at[i], pool_recv.at[i], (ahead, band))
        for i, span in enumerate(QUARTERS)
    ]
    onward = [remote(occ1, occ2, next_send.at[4], next_recv.at[4], (k, band_up))]
    onward += [
        remote(piece(first, span), piece(second, span), next_send.at[i], next_recv.at[i], (k, band_up))
        for i, span in enumerate(QUARTERS)
    ]
    ring_own = [
        ring(0, own, band, 0, x_up), ring(1, own, band, 1, x_down), ring(2, own, band, 1, x_up),
        ring(3, own, band, 0, x_down), ring(4, own, band, 0, y_mate), ring(5, own, band, 1, y_mate),
    ]
    mate_own = [to_mate(0, own, band, 0), to_mate(1, own, band, 1)]
    relays = [
        (x_down, 0, [ring(6, slots.at[x_down], x_down, 0, x_up)]),
        (x_up, 1, [ring(7, slots.at[x_up], x_up, 1, x_down)]),
        (x_down, 1, []),
        (x_up, 0, []),
        (y_mate, 0, [ring(8, slots.at[y_mate], y_mate, 0, x_up), ring(9, slots.at[y_mate], y_mate, 0, x_down)]),
        (y_mate, 1, [ring(10, slots.at[y_mate], y_mate, 1, x_up), ring(11, slots.at[y_mate], y_mate, 1, x_down)]),
        (far, 0, [ring(12, slots.at[far], far, 0, y_mate)]),
        (far, 1, [ring(13, slots.at[far], far, 1, y_mate)]),
        (other_down, 0, []), (other_down, 1, []), (other_up, 0, []), (other_up, 1, []),
        (other_far, 0, []), (other_far, 1, []),
    ]
    relays = [
        (slot, part, copies + [to_mate(2 + i, slots.at[slot], slot, part)])
        for i, (slot, part, copies) in enumerate(relays)
    ]

    def relay(*which):
        for i in which:
            slot, part, copies = relays[i]
            take(slot, part)
            for copy in copies:
                copy.start()

    def start(copies):
        for copy in copies:
            copy.start()

    start(pool)
    start(ring_own)
    start(mate_own)

    for copy in local:
        copy.wait()
    dense[:, pl.ds(360, 8), :] = jnp.zeros((2, 8, 128), F32)
    for t in range(FULL):
        dense[0, pl.ds(8 * t, 8), :] = flat[pl.ds(BLOCK * t, BLOCK)].reshape(8, 128)
    for j in range(0, TAIL, 128):
        width = min(128, TAIL - j)
        dense[0, 8 * FULL + j // 128, 0:width] = flat[pl.ds(FULL * BLOCK + j, width)]
    to_planes(dense.at[0], planes.at[0])
    permute_scale(planes.at[0], scale)
    unpack(slots.at[band], dense)
    for part in range(2):
        to_planes(dense.at[part], own_planes.at[part])
    partial[...] = jnp.zeros(partial.shape, F32)

    early = k < 2

    @pl.when(early)
    def _():
        relay(*range(14))

    @pl.when(jnp.logical_not(early))
    def _():
        relay(0, 1, 2, 3)

    for arrived, copy in zip(pool, onward):
        arrived.wait_recv()
        copy.start()

    def pair(raw, occupied):
        unpack(raw, dense)
        for part in range(2):
            to_planes(dense.at[part], planes.at[part])
        weight = -0.5 * occupied[...].astype(F32)
        return exchange_pair(own_planes, planes, weight, rows, lanes, twiddle, scale)

    @pl.when(jnp.logical_not(early))
    def _():
        relay(4, 5, 6, 7)

    re, im = pair(first, occ1)
    for part, value in enumerate((re, im)):
        accum[part, 0], accum[part, 1] = value[:, :128], value[:, 128:]

    for copy in onward:
        copy.wait_recv()
    re, im = pair(second, occ2)
    for part, value in enumerate((re, im)):
        accum[part, 0] += value[:, :128]
        accum[part, 1] += value[:, 128:]

    @pl.when(jnp.logical_not(early))
    def _():
        relay(*range(8, 14))

    for part in range(2):
        to_dense(accum.at[part], dense.at[part])

    def emit(start_at, width, value):
        span = pl.ds(start_at, width)
        value = value.astype(BF16)
        out[:, span] = value
        ket[:, span] = value.astype(F32)

    def emit_turned(start_at, width, value):
        ket_turned[:, pl.ds(start_at, width)] = value.astype(BF16).astype(F32)

    for t in range(FULL):
        both = dense[:, pl.ds(8 * t, 8), :]
        turned = jnp.concatenate([both[1:2], -both[0:1]], axis=0)
        emit(BLOCK * t, BLOCK, both.reshape(2, BLOCK))
        emit_turned(BLOCK * t, BLOCK, turned.reshape(2, BLOCK))
    for j in range(0, TAIL, 128):
        width = min(128, TAIL - j)
        both = dense[:, 8 * FULL + j // 128, 0:width]
        emit(FULL * BLOCK + j, width, both)
        emit_turned(FULL * BLOCK + j, width, jnp.concatenate([both[1:2], -both[0:1]], axis=0))

    def overlap(slot):
        for index, side in ((slot, ket), (slot + n_band, ket_turned)):
            total = jnp.zeros((2, BLOCK), F32)
            for t in range(FULL):
                span = pl.ds(BLOCK * t, BLOCK)
                total += slots[slot, :, span].astype(F32) * side[:, span]
            fold = total[:, 0:128]
            for j in range(1, BLOCK // 128):
                fold += total[:, 128 * j : 128 * j + 128]
            for j in range(0, TAIL - 64, 128):
                span = pl.ds(FULL * BLOCK + j, 128)
                fold += slots[slot, :, span].astype(F32) * side[:, span]
            span = pl.ds(GRID - 64, 64)
            partial[index, 0:2, :] = fold
            partial[index, 2:4, 0:64] = slots[slot, :, span].astype(F32) * side[:, span]

    def same(j, carry):
        overlap(at((y + j // NX) % 2, (x + j) % NX, core))
        return carry

    def twin(j, carry):
        slot = at((y + j // NX) % 2, (x + j) % NX, 1 - core)
        for part in range(2):
            take(slot, part)
        overlap(slot)
        return carry

    lax.fori_loop(0, 2 * NX, same, 0)
    lax.fori_loop(0, 2 * NX, twin, 0)

    sums = partial[...].sum(axis=1)
    ones = jnp.full((8, 128), 1.0 / math.sqrt(GRID), F32)
    line = lax.dot_general(
        ones, sums, (((1,), (1,)), ((), ())), precision=lax.Precision.HIGHEST, preferred_element_type=F32
    )
    gram[0] = line[0:1, 0:n_band]
    gram[1] = line[0:1, n_band : 2 * n_band]

    for copy in pool + onward + ring_own + mate_own:
        copy.wait_send()
    for _, _, copies in relays:
        for copy in copies:
            copy.wait_send()


def shards(n_pool, orbitals, occupation, kernel):
    n_band = 4 * NX
    vmem = pl.BlockSpec(memory_space=pltpu.VMEM)
    hbm = pl.BlockSpec(memory_space=pltpu.HBM)
    raw = pltpu.VMEM((2, GRID), BF16)
    dma = pltpu.SemaphoreType.DMA
    scalar = pltpu.VMEM((1, 1), jnp.int32)
    plane = pltpu.VMEM((2, 2, SIDE, 128), F32)
    exchanged, gram = pl.pallas_call(
        functools.partial(kernel_body, n_pool),
        out_shape=(
            jax.ShapeDtypeStruct((2, GRID), BF16),
            jax.ShapeDtypeStruct((2, 1, n_band), F32),
        ),
        in_specs=[hbm, vmem, hbm, hbm, hbm, hbm],
        out_specs=(vmem, vmem),
        scratch_shapes=[
            raw, raw, scalar, scalar,
            pltpu.VMEM((n_band, 2, GRID), BF16),
            pltpu.VMEM((GRID,), F32),
            pltpu.VMEM((2, SIDE, SIDE), BF16),
            pltpu.VMEM((2, WIDE, WIDE), BF16),
            pltpu.VMEM((2, SIDE, WIDE), F32),
            pltpu.VMEM((2, DENSE, 128), F32),
            plane, plane, plane,
            pltpu.VMEM((2, SIDE, 128), F32),
            pltpu.VMEM((2, GRID), F32),
            pltpu.VMEM((2, GRID), F32),
            pltpu.VMEM((2 * n_band, 8, 128), F32),
            dma((5,)), dma((5,)), dma((5,)), dma((5,)), dma((5,)), dma((n_band, 2)), dma((14,)), dma((16,)),
        ],
        compiler_params=pltpu.CompilerParams(
            collective_id=0, has_side_effects=True, vmem_limit_bytes=67043328
        ),
    )(orbitals.reshape(2, GRID), occupation, kernel, *tables())
    return exchanged.reshape(1, 1, 2, GRID), gram.reshape(1, 2, n_band, 1)


def solution(mesh):
    return jax.shard_map(
        functools.partial(shards, mesh.shape["pool"]),
        mesh=mesh,
        in_specs=(P("pool", "band", None, None), P("pool", "band"), P()),
        out_specs=(P("pool", "band", None, None), P("pool", None, None, "band")),
        check_vma=False,
    )
```

time: 42.7 us -> 36.4 us (0.85)
  the two profiles are of different devices: /device:TPU:1 before, /device:TPU:18 now
where the time goes in v2:
time: 36.4 us; the launch traced here: 36.2 us
  Pallas kernels  32.6 us (90%)
  local copies, waits for them, and re-layouts  2.29 us (6%)
  between operations  1.29 us (4%)
    pallas_call x1, Pallas kernels, shards(): pl.pallas_call(functools.partial(kernel_body, n_pool), out_shape=(jax.Sha...  32.6 us
    unnamed x4, local copies, waits for them, and re-layouts  2.29 us

profile of v2, /device:TPU:18, one launch (start us, length us, event | category | flops | bytes accessed | tf_op | source)
XLA Modules:
  0.0 36.2 jit_solution(2134814254293090623)
XLA Ops:
  1.3 32.6 %shard_map.77 = (bf16[2,46656]{1,0:T(2,128)(2,1)}, f32[2,1,16]{2,1,0:T(1,128)}) custom-call(bf16[2,46656]{1,0:T(2,128)(2,1)} %bitcast.5, s32[1,1]{1,0:T(1,128)S(6)} %copy.11.occ, f32[46656]{0:T(1024)} %kernel.1, bf16[2,216,216]{2,1,0:T(8,128)(2,1)} %constant.11.rows_in, bf16[2,256,256]{2,1,0:T(8,128)(2,1)} %constant.12.lanes_in, ...), custom_call_target="tpu_custom_call" | custom-call | tf_op jit(solution)/shard_map/pallas_call | solution.py:383
  33.9 0.0 copy-start
  33.9 1.7 %copy.12 = bf16[1,1,2,46656]{3,2,1,0:T(2,128)(2,1)} copy(bf16[1,1,2,46656]{3,2,1,0:T(2,128)(2,1)} %bitcast.6) | data formatting | bytes 373248
  35.7 0.0 copy-done
  35.7 0.6 %copy.13 = f32[1,2,16,1]{2,3,1,0:T(1,128)} copy(f32[1,2,16,1]{2,3,1,0:T(1,128)S(1)} %bitcast.7) | data formatting | bytes 256
Async XLA Ops:
  33.9 1.7 %copy-start = (f32[2,1,16]{2,1,0:T(1,128)S(1)}, f32[2,1,16]{2,1,0:T(1,128)}, u32[]{:S(2)}) copy-start(f32[2,1,16]{2,1,0:T(1,128)} %get-tuple-element.5) | copy-start | bytes 388

commit v3 on v2

v3 whole, which is shorter than its diff:
```python
import functools
import math
import jax
import jax.numpy as jnp
import numpy as np
from jax import lax
from jax.experimental import pallas as pl
from jax.experimental.pallas import tpu as pltpu
from jax.sharding import PartitionSpec as P
NG = 36
GRID = 46656
SIDE = 216
WIDE = 256
DENSE = 368
BLOCK = 1024
FULL = GRID // BLOCK
TAIL = GRID - FULL * BLOCK
NX = 4
WAYS = 4
ROOM = 50331648
F32 = jnp.float32
BF16 = jnp.bfloat16
HALVES = ((0, 23296), (23296, 23360))
QUARTERS = ((0, 11648), (11648, 11648), (23296, 11648), (34944, 11712))

def tables():
    index = np.arange(SIDE)
    x, y_high = (index // 6, index % 6)
    rows = (np.outer(x, x) + 6 * np.outer(y_high, y_high)) % NG
    y_low, z = (index // NG, index % NG)
    lanes = (np.outer(z, z) + 6 * np.outer(y_low, y_low)) % NG
    twiddle = np.outer(y_high, y_low) % NG
    step = 2.0 * math.pi / NG

    def both(phases, shape):
        out = np.zeros((2,) + shape, np.float32)
        out[:, :SIDE, :SIDE] = np.stack([np.cos(step * phases), np.sin(step * phases)])
        return jnp.asarray(out)
    return (both(rows, (SIDE, SIDE)).astype(BF16), both(lanes, (WIDE, WIDE)).astype(BF16), both(twiddle, (SIDE, WIDE)))

def dot(a, b):
    return jnp.dot(a, b, preferred_element_type=F32)

def lane_index(rows):
    return lax.broadcasted_iota(jnp.int32, (rows, 128), 1)

def unpack(raw, dense):
    for t in range(FULL):
        dense[:, pl.ds(8 * t, 8), :] = raw[:, pl.ds(BLOCK * t, BLOCK)].astype(F32).reshape(2, 8, 128)
    for j in range(0, TAIL, 128):
        width = min(128, TAIL - j)
        dense[:, 8 * FULL + j // 128, 0:width] = raw[:, pl.ds(FULL * BLOCK + j, width)].astype(F32)

def to_planes(dense, planes):
    for start in range(16):
        count = 14 if start < 8 else 13
        row, shift = (SIDE * start // 128, SIDE * start % 128)
        low = dense[pl.ds(row, count, stride=27), :]
        high = dense[pl.ds(row + 1, count, stride=27), :]
        if shift:
            low, high = (pltpu.roll(low, 128 - shift, 1), pltpu.roll(high, 128 - shift, 1))
            keep = lane_index(count) < 128 - shift
            low = jnp.where(keep, low, high)
            if shift + SIDE > 256:
                last = pltpu.roll(dense[pl.ds(row + 2, count, stride=27), :], 128 - shift, 1)
                high = jnp.where(keep, high, last)
        planes[0, pl.ds(start, count, stride=16), :] = low
        planes[1, pl.ds(start, count, stride=16), :] = high

def to_dense(planes, dense):
    for q in range(27):
        count = 14 if q <= 12 else 13
        total, lane = (None, lane_index(count))
        pos = 0
        while pos < 128:
            row, col = divmod(128 * q + pos, SIDE)
            plane, first = (0, 0) if col < 128 else (1, 128)
            width = min((SIDE if plane else 128) - col, 128 - pos)
            piece = planes[plane, pl.ds(row, count, stride=16), :]
            shift = (pos - (col - first)) % 128
            if shift:
                piece = pltpu.roll(piece, shift, 1)
            total = piece if total is None else jnp.where(lane < pos, total, piece)
            pos += width
        dense[pl.ds(q, count, stride=27), :] = total
    row, col = divmod(364 * 128, SIDE)
    dense[364:365, 0:64] = planes[1, row:row + 1, col - 128:col - 64]

def permute_scale(planes, scale):
    lane = lane_index(NG)
    for low in range(6):
        for plane in range(2):
            total = jnp.zeros((NG, 128), F32)
            for high in range(6):
                pos, end = (max(NG * high, 128 * plane), min(NG * high + NG, 128 * plane + 128))
                while pos < end:
                    col = NG * low + pos - NG * high
                    source = col // 128
                    width = min(end - pos, 128 * (source + 1) - col)
                    piece = planes[source, pl.ds(high, NG, stride=6), :]
                    shift = (pos - col) % 128
                    if shift:
                        piece = pltpu.roll(piece, shift, 1)
                    at = pos - 128 * plane
                    total = jnp.where((lane >= at) & (lane < at + width), piece, total)
                    pos += width
            scale[plane, pl.ds(low, NG, stride=6), :] = total * (1.0 / GRID)

def wide(planes):
    return jnp.concatenate([planes[0], planes[1]], axis=1)

def exchange_pair(own, other, weight, rows, lanes, twiddle, scale):
    c, d, a, b = (wide(own.at[0]), wide(own.at[1]), wide(other.at[0]), wide(other.at[1]))
    re, im = ((a * c + b * d).astype(BF16), (a * d - b * c).astype(BF16))
    cos, sin = (rows[0], rows[1])
    turn_re, turn_im = (twiddle[0], twiddle[1])
    u, v = (dot(cos, re) + dot(sin, im), dot(cos, im) - dot(sin, re))
    re, im = ((u * turn_re + v * turn_im).astype(BF16), (v * turn_re - u * turn_im).astype(BF16))
    cos, sin = (lanes[0], lanes[1])
    factor = wide(scale)
    u, v = (dot(re, cos) + dot(im, sin), dot(im, cos) - dot(re, sin))
    re, im = ((u * factor).astype(BF16), (v * factor).astype(BF16))
    u, v = (dot(re, cos) - dot(im, sin), dot(im, cos) + dot(re, sin))
    re, im = ((u * turn_re - v * turn_im).astype(BF16), (v * turn_re + u * turn_im).astype(BF16))
    cos, sin = (rows[0], rows[1])
    e, f = (dot(cos, re) - dot(sin, im), dot(cos, im) + dot(sin, re))
    return (weight * (a * e - b * f), weight * (a * f + b * e))

def kernel_body(n_pool, own, occ, kernel, rows_in, lanes_in, twiddle_in, accum, slots, first, second, occ1, occ2, flat, rows, lanes, twiddle, dense, own_planes, planes, scale, local_sem, pool_send, pool_recv, next_send, next_recv, slot_recv, ring_send, mate_send):
    k, band = (lax.axis_index('pool'), lax.axis_index('band'))
    n_band = 4 * NX
    y, x, core = (band // (2 * NX), band // 2 % NX, band % 2)

    def at(yy, xx, cc):
        return yy * (2 * NX) + xx * 2 + cc
    ahead, behind = ((k + 1) % n_pool, (k + n_pool - 1) % n_pool)
    right, left, across = ((x + 1) % NX, (x + NX - 1) % NX, (x + 2) % NX)
    x_up, x_down = (at(y, right, core), at(y, left, core))
    y_mate, mate = (at(1 - y, x, core), at(y, x, 1 - core))
    band_up, band_down = ((band + 1) % n_band, (band + n_band - 1) % n_band)
    mesh_id = pl.DeviceIdType.MESH
    barrier = pltpu.get_barrier_semaphore()
    senders = [(behind, band)] + [(k, b) for b in (band_down, x_up, x_down, y_mate, mate)]
    for device in senders:
        pl.semaphore_signal(barrier, inc=1, device_id=device, device_id_type=mesh_id)
    local = [pltpu.make_async_copy(src, dst, local_sem.at[i]) for i, (src, dst) in enumerate([(own, slots.at[band]), (kernel, flat), (rows_in, rows), (lanes_in, lanes), (twiddle_in, twiddle)])]
    for copy in local:
        copy.start()
    pl.semaphore_wait(barrier, len(senders))

    def remote(src, dst, send_sem, recv_sem, device):
        return pltpu.make_async_remote_copy(src_ref=src, dst_ref=dst, send_sem=send_sem, recv_sem=recv_sem, device_id=device, device_id_type=mesh_id)

    def piece(ref, span):
        return ref.at[:, pl.ds(span[0], span[1])]

    def ring(index, src, slot, part, to):
        span = HALVES[part]
        return remote(piece(src, span), piece(slots.at[slot], span), ring_send.at[index], slot_recv.at[slot, part], (k, to))

    def to_mate(index, src, slot, part):
        span = HALVES[part]
        return remote(piece(src, span), piece(slots.at[slot], span), mate_send.at[index], slot_recv.at[slot, part], (k, mate))

    def take(slot, part):
        ring(0, slots.at[slot], slot, part, band).wait_recv()
    other_down, other_up = (at(1 - y, left, core), at(1 - y, right, core))
    far, other_far = (at(y, across, core), at(1 - y, across, core))
    pool = [remote(occ, occ1, pool_send.at[4], pool_recv.at[4], (ahead, band))]
    pool += [remote(piece(own, span), piece(first, span), pool_send.at[i], pool_recv.at[i], (ahead, band)) for i, span in enumerate(QUARTERS)]
    onward = [remote(occ1, occ2, next_send.at[4], next_recv.at[4], (k, band_up))]
    onward += [remote(piece(first, span), piece(second, span), next_send.at[i], next_recv.at[i], (k, band_up)) for i, span in enumerate(QUARTERS)]
    ring_own = [ring(0, own, band, 0, x_up), ring(1, own, band, 1, x_down), ring(2, own, band, 1, x_up), ring(3, own, band, 0, x_down), ring(4, own, band, 0, y_mate), ring(5, own, band, 1, y_mate)]
    mate_own = [to_mate(0, own, band, 0), to_mate(1, own, band, 1)]
    relays = [(x_down, 0, [ring(6, slots.at[x_down], x_down, 0, x_up)]), (x_up, 1, [ring(7, slots.at[x_up], x_up, 1, x_down)]), (x_down, 1, []), (x_up, 0, []), (y_mate, 0, [ring(8, slots.at[y_mate], y_mate, 0, x_up), ring(9, slots.at[y_mate], y_mate, 0, x_down)]), (y_mate, 1, [ring(10, slots.at[y_mate], y_mate, 1, x_up), ring(11, slots.at[y_mate], y_mate, 1, x_down)]), (far, 0, [ring(12, slots.at[far], far, 0, y_mate)]), (far, 1, [ring(13, slots.at[far], far, 1, y_mate)]), (other_down, 0, []), (other_down, 1, []), (other_up, 0, []), (other_up, 1, []), (other_far, 0, []), (other_far, 1, [])]
    relays = [(slot, part, copies + [to_mate(2 + i, slots.at[slot], slot, part)]) for i, (slot, part, copies) in enumerate(relays)]

    def relay(*which):
        for i in which:
            slot, part, copies = relays[i]
            take(slot, part)
            for copy in copies:
                copy.start()
    twins = [(at(yy, xx, 1 - core), part) for yy in (y, 1 - y) for xx in (x, left, right, across) for part in range(2)]

    def start(copies):
        for copy in copies:
            copy.start()
    start(pool)
    start(ring_own)
    start(mate_own)
    for copy in local:
        copy.wait()
    dense[:, pl.ds(360, 8), :] = jnp.zeros((2, 8, 128), F32)
    for t in range(FULL):
        dense[0, pl.ds(8 * t, 8), :] = flat[pl.ds(BLOCK * t, BLOCK)].reshape(8, 128)
    for j in range(0, TAIL, 128):
        width = min(128, TAIL - j)
        dense[0, 8 * FULL + j // 128, 0:width] = flat[pl.ds(FULL * BLOCK + j, width)]
    to_planes(dense.at[0], planes.at[0])
    permute_scale(planes.at[0], scale)
    unpack(slots.at[band], dense)
    for part in range(2):
        to_planes(dense.at[part], own_planes.at[part])
    early = k == 0

    @pl.when(early)
    def _():
        relay(*range(8))

    @pl.when(jnp.logical_not(early))
    def _():
        relay(0, 1, 2, 3)
    for arrived, copy in zip(pool, onward):
        arrived.wait_recv()
        copy.start()

    def pair(raw, occupied):
        unpack(raw, dense)
        for part in range(2):
            to_planes(dense.at[part], planes.at[part])
        weight = -0.5 * occupied[...].astype(F32)
        return exchange_pair(own_planes, planes, weight, rows, lanes, twiddle, scale)

    @pl.when(jnp.logical_not(early))
    def _():
        relay(*(4, 5, 6, 7))
    re, im = pair(first, occ1)
    for part, value in enumerate((re, im)):
        accum[part, 0], accum[part, 1] = (value[:, :128], value[:, 128:])
    for copy in onward:
        copy.wait_recv()
    re, im = pair(second, occ2)
    for part, value in enumerate((re, im)):
        accum[part, 0] += value[:, :128]
        accum[part, 1] += value[:, 128:]
    relay(*range(8, 14))
    for slot, part in twins:
        take(slot, part)
    for copy in pool:
        copy.wait_send()
    for copy in onward + ring_own + mate_own:
        copy.wait_send()
    for _, _, copies in relays:
        for copy in copies:
            copy.wait_send()

def finish_body(accum, slots, out_hbm, gram, out, dense, ket, ket_turned, partial, sem):
    n_band = slots.shape[0]
    for part in range(2):
        to_dense(accum.at[part], dense.at[part])
    partial[...] = jnp.zeros(partial.shape, F32)

    def emit(start_at, width, value):
        span = pl.ds(start_at, width)
        value = value.astype(BF16)
        out[:, span] = value
        ket[:, span] = value.astype(F32)

    def emit_turned(start_at, width, value):
        ket_turned[:, pl.ds(start_at, width)] = value.astype(BF16).astype(F32)
    for t in range(FULL):
        both = dense[:, pl.ds(8 * t, 8), :]
        turned = jnp.concatenate([both[1:2], -both[0:1]], axis=0)
        emit(BLOCK * t, BLOCK, both.reshape(2, BLOCK))
        emit_turned(BLOCK * t, BLOCK, turned.reshape(2, BLOCK))
    for j in range(0, TAIL, 128):
        width = min(128, TAIL - j)
        both = dense[:, 8 * FULL + j // 128, 0:width]
        emit(FULL * BLOCK + j, width, both)
        emit_turned(FULL * BLOCK + j, width, jnp.concatenate([both[1:2], -both[0:1]], axis=0))
    result = pltpu.make_async_copy(out, out_hbm, sem)
    result.start()

    def overlap(step, carry):
        pair = [2 * step, 2 * step + 1]
        totals = [[jnp.zeros((2, BLOCK), F32) for _ in range(WAYS)] for _ in range(4)]
        for t in range(FULL):
            span = pl.ds(BLOCK * t, BLOCK)
            sides = (ket[:, span], ket_turned[:, span])
            for s, slot in enumerate(pair):
                value = slots[slot, :, span].astype(F32)
                for i, side in enumerate(sides):
                    totals[2 * s + i][t % WAYS] += value * side
        for s, slot in enumerate(pair):
            for i, side in enumerate((ket, ket_turned)):
                index = slot + n_band * i
                total = sum(totals[2 * s + i][1:], totals[2 * s + i][0])
                fold = total[:, 0:128]
                for j in range(1, BLOCK // 128):
                    fold += total[:, 128 * j:128 * j + 128]
                for j in range(0, TAIL - 64, 128):
                    span = pl.ds(FULL * BLOCK + j, 128)
                    fold += slots[slot, :, span].astype(F32) * side[:, span]
                span = pl.ds(GRID - 64, 64)
                partial[index, 0:2, :] = fold
                partial[index, 2:4, 0:64] = slots[slot, :, span].astype(F32) * side[:, span]
        return carry
    lax.fori_loop(0, n_band // 2, overlap, 0)
    sums = partial[...].sum(axis=1)
    ones = jnp.full((8, 128), 1.0 / math.sqrt(GRID), F32)
    line = lax.dot_general(ones, sums, (((1,), (1,)), ((), ())), precision=lax.Precision.HIGHEST, preferred_element_type=F32)
    gram[0] = line[0:1, 0:n_band]
    gram[1] = line[0:1, n_band:2 * n_band]
    result.wait()

def pin(value):
    return pltpu.with_memory_space_constraint(value, pltpu.HBM)

def shards(n_pool, orbitals, occupation, kernel):
    n_band = 4 * NX
    vmem = pl.BlockSpec(memory_space=pltpu.VMEM)
    hbm = pl.BlockSpec(memory_space=pltpu.HBM)
    raw = pltpu.VMEM((2, GRID), BF16)
    dma = pltpu.SemaphoreType.DMA
    scalar = pltpu.VMEM((1, 1), jnp.int32)
    plane = pltpu.VMEM((2, 2, SIDE, 128), F32)
    accum, slots = pl.pallas_call(functools.partial(kernel_body, n_pool), out_shape=(jax.ShapeDtypeStruct((2, 2, SIDE, 128), F32), jax.ShapeDtypeStruct((n_band, 2, GRID), BF16)), in_specs=[hbm] * 6, out_specs=(vmem, vmem), scratch_shapes=[raw, raw, scalar, scalar, pltpu.VMEM((GRID,), F32), pltpu.VMEM((2, SIDE, SIDE), BF16), pltpu.VMEM((2, WIDE, WIDE), BF16), pltpu.VMEM((2, SIDE, WIDE), F32), pltpu.VMEM((2, DENSE, 128), F32), plane, plane, pltpu.VMEM((2, SIDE, 128), F32), dma((5,)), dma((5,)), dma((5,)), dma((5,)), dma((5,)), dma((n_band, 2)), dma((14,)), dma((16,))], compiler_params=pltpu.CompilerParams(collective_id=0, has_side_effects=True, vmem_limit_bytes=ROOM), name='exchange')(pin(orbitals.reshape(2, GRID)), occupation, *map(pin, (kernel, *tables())))
    exchanged, gram = pl.pallas_call(finish_body, out_shape=(jax.ShapeDtypeStruct((2, GRID), BF16), jax.ShapeDtypeStruct((2, 1, n_band), F32)), in_specs=[vmem, vmem], out_specs=(hbm, vmem), scratch_shapes=[raw, pltpu.VMEM((2, DENSE, 128), F32), pltpu.VMEM((2, GRID), F32), pltpu.VMEM((2, GRID), F32), pltpu.VMEM((2 * n_band, 8, 128), F32), dma], compiler_params=pltpu.CompilerParams(vmem_limit_bytes=16 * 1024 * 1024), name='finish')(accum, slots)
    return (exchanged.reshape(1, 1, 2, GRID), gram.reshape(1, 2, n_band, 1))

def solution(mesh):
    return jax.shard_map(functools.partial(shards, mesh.shape['pool']), mesh=mesh, in_specs=(P('pool', 'band', None, None), P('pool', 'band'), P()), out_specs=(P('pool', 'band', None, None), P('pool', None, None, 'band')), check_vma=False)
```

time: 36.4 us -> 32.2 us (0.88)
  the two profiles are of different devices: /device:TPU:18 before, /device:TPU:1 now
where the time goes in v3:
time: 32.2 us; the launch traced here: 32 us
  Pallas kernels  30.7 us (95%)
  between operations  1.28 us (4%)
    pallas_call x1, Pallas kernels, shards(): pl.pallas_call(functools.partial(kernel_body, n_pool), out_shape=(jax.Sha...  27.7 us
    pallas_call x1, Pallas kernels, shards(): pl.pallas_call(finish_body, out_shape=(jax.ShapeDtypeStruct((2, GRID), BF...  3.03 us

profile of v3, /device:TPU:1, one launch (start us, length us, event | category | flops | bytes accessed | tf_op | source)
XLA Modules:
  0.0 32.0 jit_solution(7007125766066833303)
XLA Ops:
  1.3 27.7 %exchange.1 = (f32[2,2,216,128]{3,2,1,0:T(8,128)S(1)}, bf16[16,2,46656]{2,1,0:T(2,128)(2,1)S(1)}) custom-call(bf16[2,46656]{1,0:T(2,128)(2,1)} %bitcast.5, s32[1,1]{1,0:T(1,128)S(6)} %copy.9.occ, f32[46656]{0:T(1024)} %kernel.1, bf16[2,216,216]{2,1,0:T(8,128)(2,1)} %constant.11.rows_in, bf16[2,256,256]{2,1,0:T(8,128)(2,1)} %constant.12.lanes_in, ...), custom_call_target="tpu_custom_call" | custom-call | tf_op jit(solution)/shard_map/exchange/pallas_call | solution.py:318
  29.0 3.0 %finish.1 = (bf16[2,46656]{1,0:T(2,128)(2,1)}, f32[2,1,16]{2,1,0:T(1,128)}) custom-call(f32[2,2,216,128]{3,2,1,0:T(8,128)S(1)} %get-tuple-element.6.accum, bf16[16,2,46656]{2,1,0:T(2,128)(2,1)S(1)} %get-tuple-element.7.slots), custom_call_target="tpu_custom_call" | custom-call | tf_op jit(solution)/shard_map/finish/pallas_call | solution.py:319

commit v4 on v3

--- a/solution.py
+++ b/solution.py
@@ -186,8 +186,17 @@
     def start(copies):
         for copy in copies:
             copy.start()
-    start(pool)
-    start(ring_own)
+    early = k == 0
+
+    @pl.when(jnp.logical_not(early))
+    def _():
+        start(pool)
+    start(ring_own[4:])
+    start(ring_own[:4])
+
+    @pl.when(early)
+    def _():
+        start(pool)
     start(mate_own)
     for copy in local:
         copy.wait()
@@ -202,7 +211,6 @@
     unpack(slots.at[band], dense)
     for part in range(2):
         to_planes(dense.at[part], own_planes.at[part])
-    early = k == 0
 
     @pl.when(early)
     def _():
@@ -228,13 +236,20 @@
     re, im = pair(first, occ1)
     for part, value in enumerate((re, im)):
         accum[part, 0], accum[part, 1] = (value[:, :128], value[:, 128:])
+
+    @pl.when(early)
+    def _():
+        relay(*range(8, 14))
     for copy in onward:
         copy.wait_recv()
     re, im = pair(second, occ2)
     for part, value in enumerate((re, im)):
         accum[part, 0] += value[:, :128]
         accum[part, 1] += value[:, 128:]
-    relay(*range(8, 14))
+
+    @pl.when(jnp.logical_not(early))
+    def _():
+        relay(*range(8, 14))
     for slot, part in twins:
         take(slot, part)
     for copy in pool:

time: 32.2 us -> 30.7 us (0.953)
  Pallas kernels: 30.7 us -> 29.3 us
    pallas_call x1, Pallas kernels: 27.7 us -> 26.2 us  [shards(): pl.pallas_call(functools.partial(kernel_body, n_pool), out_shape=(jax.Sha...]
where the time goes in v4:
time: 30.7 us; the launch traced here: 30.6 us
  Pallas kernels  29.3 us (95%)
  between operations  1.28 us (4%)
    pallas_call x1, Pallas kernels, shards(): pl.pallas_call(functools.partial(kernel_body, n_pool), out_shape=(jax.Sha...  26.2 us
    pallas_call x1, Pallas kernels, shards(): pl.pallas_call(finish_body, out_shape=(jax.ShapeDtypeStruct((2, GRID), BF...  3.03 us

profile of v4, /device:TPU:1, one launch (start us, length us, event | category | flops | bytes accessed | tf_op | source)
XLA Modules:
  0.0 30.6 jit_solution(9663641622016768267)
XLA Ops:
  1.3 26.2 %exchange.1 = (f32[2,2,216,128]{3,2,1,0:T(8,128)S(1)}, bf16[16,2,46656]{2,1,0:T(2,128)(2,1)S(1)}) custom-call(bf16[2,46656]{1,0:T(2,128)(2,1)} %bitcast.5, s32[1,1]{1,0:T(1,128)S(6)} %copy.9.occ, f32[46656]{0:T(1024)} %kernel.1, bf16[2,216,216]{2,1,0:T(8,128)(2,1)} %constant.11.rows_in, bf16[2,256,256]{2,1,0:T(8,128)(2,1)} %constant.12.lanes_in, ...), custom_call_target="tpu_custom_call" | custom-call | tf_op jit(solution)/shard_map/exchange/pallas_call | solution.py:333
  27.5 3.0 %finish.1 = (bf16[2,46656]{1,0:T(2,128)(2,1)}, f32[2,1,16]{2,1,0:T(1,128)}) custom-call(f32[2,2,216,128]{3,2,1,0:T(8,128)S(1)} %get-tuple-element.6.accum, bf16[16,2,46656]{2,1,0:T(2,128)(2,1)S(1)} %get-tuple-element.7.slots), custom_call_target="tpu_custom_call" | custom-call | tf_op jit(solution)/shard_map/finish/pallas_call | solution.py:334

commit v5 on v4

--- a/solution.py
+++ b/solution.py
@@ -126,7 +126,7 @@
     e, f = (dot(cos, re) - dot(sin, im), dot(cos, im) + dot(sin, re))
     return (weight * (a * e - b * f), weight * (a * f + b * e))
 
-def kernel_body(n_pool, own, occ, kernel, rows_in, lanes_in, twiddle_in, accum, slots, first, second, occ1, occ2, flat, rows, lanes, twiddle, dense, own_planes, planes, scale, local_sem, pool_send, pool_recv, next_send, next_recv, slot_recv, ring_send, mate_send):
+def kernel_body(n_pool, own, occ, kernel, rows_in, lanes_in, twiddle_in, out, ket, ket_turned, partial, slots, first, second, occ1, occ2, flat, rows, lanes, twiddle, dense, own_planes, planes, accum, scale, local_sem, pool_send, pool_recv, next_send, next_recv, slot_recv, ring_send, mate_send):
     k, band = (lax.axis_index('pool'), lax.axis_index('band'))
     n_band = 4 * NX
     y, x, core = (band // (2 * NX), band // 2 % NX, band % 2)
@@ -250,6 +250,14 @@
     @pl.when(jnp.logical_not(early))
     def _():
         relay(*range(8, 14))
+    emit_result(accum, dense, out, ket, ket_turned)
+    partial[...] = jnp.zeros(partial.shape, F32)
+
+    def same(step, carry):
+        pair = [4 * step + core, 4 * step + 2 + core]
+        overlap(pair, pair, slots, ket, ket_turned, partial)
+        return carry
+    lax.fori_loop(0, n_band // 4, same, 0)
     for slot, part in twins:
         take(slot, part)
     for copy in pool:
@@ -260,58 +268,61 @@
         for copy in copies:
             copy.wait_send()
 
-def finish_body(accum, slots, out_hbm, gram, out, dense, ket, ket_turned, partial, sem):
-    n_band = slots.shape[0]
+def emit_result(accum, dense, out, ket, ket_turned):
     for part in range(2):
         to_dense(accum.at[part], dense.at[part])
-    partial[...] = jnp.zeros(partial.shape, F32)
-
-    def emit(start_at, width, value):
+
+    def emit(start_at, width, value, turned):
         span = pl.ds(start_at, width)
         value = value.astype(BF16)
         out[:, span] = value
         ket[:, span] = value.astype(F32)
-
-    def emit_turned(start_at, width, value):
-        ket_turned[:, pl.ds(start_at, width)] = value.astype(BF16).astype(F32)
+        ket_turned[:, span] = turned.astype(BF16).astype(F32)
     for t in range(FULL):
         both = dense[:, pl.ds(8 * t, 8), :]
         turned = jnp.concatenate([both[1:2], -both[0:1]], axis=0)
-        emit(BLOCK * t, BLOCK, both.reshape(2, BLOCK))
-        emit_turned(BLOCK * t, BLOCK, turned.reshape(2, BLOCK))
+        emit(BLOCK * t, BLOCK, both.reshape(2, BLOCK), turned.reshape(2, BLOCK))
     for j in range(0, TAIL, 128):
         width = min(128, TAIL - j)
         both = dense[:, 8 * FULL + j // 128, 0:width]
-        emit(FULL * BLOCK + j, width, both)
-        emit_turned(FULL * BLOCK + j, width, jnp.concatenate([both[1:2], -both[0:1]], axis=0))
+        turned = jnp.concatenate([both[1:2], -both[0:1]], axis=0)
+        emit(FULL * BLOCK + j, width, both, turned)
+
+def overlap(pair, places, slots, ket, ket_turned, partial):
+    totals = [[jnp.zeros((2, BLOCK), F32) for _ in range(WAYS)] for _ in range(4)]
+    for t in range(FULL):
+        span = pl.ds(BLOCK * t, BLOCK)
+        sides = (ket[:, span], ket_turned[:, span])
+        for s, slot in enumerate(pair):
+            value = slots[slot, :, span].astype(F32)
+            for i, side in enumerate(sides):
+                totals[2 * s + i][t % WAYS] += value * side
+    for s, slot in enumerate(pair):
+        for i, side in enumerate((ket, ket_turned)):
+            index = places[s] + partial.shape[0] // 2 * i
+            total = sum(totals[2 * s + i][1:], totals[2 * s + i][0])
+            fold = total[:, 0:128]
+            for j in range(1, BLOCK // 128):
+                fold += total[:, 128 * j:128 * j + 128]
+            for j in range(0, TAIL - 64, 128):
+                span = pl.ds(FULL * BLOCK + j, 128)
+                fold += slots[slot, :, span].astype(F32) * side[:, span]
+            span = pl.ds(GRID - 64, 64)
+            partial[index, 0:2, :] = fold
+            partial[index, 2:4, 0:64] = slots[slot, :, span].astype(F32) * side[:, span]
+
+def finish_body(out, ket, ket_turned, half, slots, out_hbm, gram, partial, sem):
+    n_band = slots.shape[0]
+    core = lax.axis_index('band') % 2
     result = pltpu.make_async_copy(out, out_hbm, sem)
     result.start()
-
-    def overlap(step, carry):
-        pair = [2 * step, 2 * step + 1]
-        totals = [[jnp.zeros((2, BLOCK), F32) for _ in range(WAYS)] for _ in range(4)]
-        for t in range(FULL):
-            span = pl.ds(BLOCK * t, BLOCK)
-            sides = (ket[:, span], ket_turned[:, span])
-            for s, slot in enumerate(pair):
-                value = slots[slot, :, span].astype(F32)
-                for i, side in enumerate(sides):
-                    totals[2 * s + i][t % WAYS] += value * side
-        for s, slot in enumerate(pair):
-            for i, side in enumerate((ket, ket_turned)):
-                index = slot + n_band * i
-                total = sum(totals[2 * s + i][1:], totals[2 * s + i][0])
-                fold = total[:, 0:128]
-                for j in range(1, BLOCK // 128):
-                    fold += total[:, 128 * j:128 * j + 128]
-                for j in range(0, TAIL - 64, 128):
-                    span = pl.ds(FULL * BLOCK + j, 128)
-                    fold += slots[slot, :, span].astype(F32) * side[:, span]
-                span = pl.ds(GRID - 64, 64)
-                partial[index, 0:2, :] = fold
-                partial[index, 2:4, 0:64] = slots[slot, :, span].astype(F32) * side[:, span]
+    partial[...] = half[...]
+
+    def twin(step, carry):
+        pair = [4 * step + 1 - core, 4 * step + 3 - core]
+        overlap(pair, pair, slots, ket, ket_turned, partial)
         return carry
-    lax.fori_loop(0, n_band // 2, overlap, 0)
+    lax.fori_loop(0, n_band // 4, twin, 0)
     sums = partial[...].sum(axis=1)
     ones = jnp.full((8, 128), 1.0 / math.sqrt(GRID), F32)
     line = lax.dot_general(ones, sums, (((1,), (1,)), ((), ())), precision=lax.Precision.HIGHEST, preferred_element_type=F32)
@@ -330,8 +341,9 @@
     dma = pltpu.SemaphoreType.DMA
     scalar = pltpu.VMEM((1, 1), jnp.int32)
     plane = pltpu.VMEM((2, 2, SIDE, 128), F32)
-    accum, slots = pl.pallas_call(functools.partial(kernel_body, n_pool), out_shape=(jax.ShapeDtypeStruct((2, 2, SIDE, 128), F32), jax.ShapeDtypeStruct((n_band, 2, GRID), BF16)), in_specs=[hbm] * 6, out_specs=(vmem, vmem), scratch_shapes=[raw, raw, scalar, scalar, pltpu.VMEM((GRID,), F32), pltpu.VMEM((2, SIDE, SIDE), BF16), pltpu.VMEM((2, WIDE, WIDE), BF16), pltpu.VMEM((2, SIDE, WIDE), F32), pltpu.VMEM((2, DENSE, 128), F32), plane, plane, pltpu.VMEM((2, SIDE, 128), F32), dma((5,)), dma((5,)), dma((5,)), dma((5,)), dma((5,)), dma((n_band, 2)), dma((14,)), dma((16,))], compiler_params=pltpu.CompilerParams(collective_id=0, has_side_effects=True, vmem_limit_bytes=ROOM), name='exchange')(pin(orbitals.reshape(2, GRID)), occupation, *map(pin, (kernel, *tables())))
-    exchanged, gram = pl.pallas_call(finish_body, out_shape=(jax.ShapeDtypeStruct((2, GRID), BF16), jax.ShapeDtypeStruct((2, 1, n_band), F32)), in_specs=[vmem, vmem], out_specs=(hbm, vmem), scratch_shapes=[raw, pltpu.VMEM((2, DENSE, 128), F32), pltpu.VMEM((2, GRID), F32), pltpu.VMEM((2, GRID), F32), pltpu.VMEM((2 * n_band, 8, 128), F32), dma], compiler_params=pltpu.CompilerParams(vmem_limit_bytes=16 * 1024 * 1024), name='finish')(accum, slots)
+    sums = pltpu.VMEM((2 * n_band, 8, 128), F32)
+    results = pl.pallas_call(functools.partial(kernel_body, n_pool), out_shape=(jax.ShapeDtypeStruct((2, GRID), BF16), jax.ShapeDtypeStruct((2, GRID), F32), jax.ShapeDtypeStruct((2, GRID), F32), jax.ShapeDtypeStruct((2 * n_band, 8, 128), F32), jax.ShapeDtypeStruct((n_band, 2, GRID), BF16)), in_specs=[hbm] * 6, out_specs=(vmem,) * 5, scratch_shapes=[raw, raw, scalar, scalar, pltpu.VMEM((GRID,), F32), pltpu.VMEM((2, SIDE, SIDE), BF16), pltpu.VMEM((2, WIDE, WIDE), BF16), pltpu.VMEM((2, SIDE, WIDE), F32), pltpu.VMEM((2, DENSE, 128), F32), plane, plane, plane, pltpu.VMEM((2, SIDE, 128), F32), dma((5,)), dma((5,)), dma((5,)), dma((5,)), dma((5,)), dma((n_band, 2)), dma((14,)), dma((16,))], compiler_params=pltpu.CompilerParams(collective_id=0, has_side_effects=True, vmem_limit_bytes=ROOM), name='exchange')(pin(orbitals.reshape(2, GRID)), occupation, *map(pin, (kernel, *tables())))
+    exchanged, gram = pl.pallas_call(finish_body, out_shape=(jax.ShapeDtypeStruct((2, GRID), BF16), jax.ShapeDtypeStruct((2, 1, n_band), F32)), in_specs=[vmem] * 5, out_specs=(hbm, vmem), scratch_shapes=[sums, dma], compiler_params=pltpu.CompilerParams(vmem_limit_bytes=16 * 1024 * 1024), name='finish')(*results)
     return (exchanged.reshape(1, 1, 2, GRID), gram.reshape(1, 2, n_band, 1))
 
 def solution(mesh):

time: 30.7 us -> 30.1 us (0.980)
  Pallas kernels: 29.3 us -> 28.7 us
    pallas_call x1, Pallas kernels: 3.03 us -> 1.5 us  [shards(): pl.pallas_call(finish_body, out_shape=(jax.ShapeDtypeStruct((2, GRID), BF...]
    pallas_call x1, Pallas kernels: 26.2 us -> 27.2 us  [shards(): pl.pallas_call(functools.partial(kernel_body, n_pool), out_shape=(jax.Sha...]
where the time goes in v5:
time: 30.1 us; the launch traced here: 30 us
  Pallas kernels  28.7 us (95%)
  between operations  1.28 us (4%)
    pallas_call x1, Pallas kernels, shards(): pl.pallas_call(functools.partial(kernel_body, n_pool), out_shape=(jax.Sha...  27.2 us
    pallas_call x1, Pallas kernels, shards(): pl.pallas_call(finish_body, out_shape=(jax.ShapeDtypeStruct((2, GRID), BF...  1.5 us

profile of v5, /device:TPU:1, one launch (start us, length us, event | category | flops | bytes accessed | tf_op | source)
XLA Modules:
  0.0 30.0 jit_solution(8871996615737724620)
XLA Ops:
  1.3 27.2 %exchange.1 = (bf16[2,46656]{1,0:T(2,128)(2,1)S(1)}, f32[2,46656]{1,0:T(2,128)S(1)}, f32[2,46656]{1,0:T(2,128)S(1)}, f32[32,8,128]{2,1,0:T(8,128)S(1)}, bf16[16,2,46656]{2,1,0:T(2,128)(2,1)S(1)}) custom-call(bf16[2,46656]{1,0:T(2,128)(2,1)} %bitcast.5, s32[1,1]{1,0:T(1,128)S(6)} %copy.9.occ, f32[46656]{0:T(1024)} %kernel.1, ...), custom_call_target="tpu_custom_call" | custom-call | tf_op jit(solution)/shard_map/exchange/pallas_call | solution.py:345
  28.5 1.5 %finish.1 = (bf16[2,46656]{1,0:T(2,128)(2,1)}, f32[2,1,16]{2,1,0:T(1,128)}) custom-call(bf16[2,46656]{1,0:T(2,128)(2,1)S(1)} %get-tuple-element.9.out, f32[2,46656]{1,0:T(2,128)S(1)} %get-tuple-element.10.ket, f32[2,46656]{1,0:T(2,128)S(1)} %get-tuple-element.11.ket_turned, f32[32,8,128]{2,1,0:T(8,128)S(1)} %get-tuple-element.12.half, ...), custom_call_target="tpu_custom_call" | custom-call | tf_op jit(solution)/shard_map/finish/pallas_call | solution.py:346

commit v6 on v5

--- a/solution.py
+++ b/solution.py
@@ -187,8 +187,10 @@
         for copy in copies:
             copy.start()
     early = k == 0
-
-    @pl.when(jnp.logical_not(early))
+    held = k == n_pool - 2
+    final = k == n_pool - 1
+
+    @pl.when(jnp.logical_not(early | held))
     def _():
         start(pool)
     start(ring_own[4:])
@@ -211,6 +213,10 @@
     unpack(slots.at[band], dense)
     for part in range(2):
         to_planes(dense.at[part], own_planes.at[part])
+
+    @pl.when(held)
+    def _():
+        start(pool)
 
     @pl.when(early)
     def _():

time: 30.1 us -> 30.1 us (level)
  no operation moved by 1% of the time
where the time goes in v6:
time: 30.1 us; the launch traced here: 30 us
  Pallas kernels  28.7 us (95%)
  between operations  1.28 us (4%)
    pallas_call x1, Pallas kernels, shards(): pl.pallas_call(functools.partial(kernel_body, n_pool), out_shape=(jax.Sha...  27.2 us
    pallas_call x1, Pallas kernels, shards(): pl.pallas_call(finish_body, out_shape=(jax.ShapeDtypeStruct((2, GRID), BF...  1.5 us

profile of v6, /device:TPU:1, one launch (start us, length us, event | category | flops | bytes accessed | tf_op | source)
XLA Modules:
  0.0 30.0 jit_solution(4559493707714344663)
XLA Ops:
  1.3 27.2 %exchange.1 = (bf16[2,46656]{1,0:T(2,128)(2,1)S(1)}, f32[2,46656]{1,0:T(2,128)S(1)}, f32[2,46656]{1,0:T(2,128)S(1)}, f32[32,8,128]{2,1,0:T(8,128)S(1)}, bf16[16,2,46656]{2,1,0:T(2,128)(2,1)S(1)}) custom-call(bf16[2,46656]{1,0:T(2,128)(2,1)} %bitcast.5, s32[1,1]{1,0:T(1,128)S(6)} %copy.9.occ, f32[46656]{0:T(1024)} %kernel.1, ...), custom_call_target="tpu_custom_call" | custom-call | tf_op jit(solution)/shard_map/exchange/pallas_call | solution.py:351
  28.5 1.5 %finish.1 = (bf16[2,46656]{1,0:T(2,128)(2,1)}, f32[2,1,16]{2,1,0:T(1,128)}) custom-call(bf16[2,46656]{1,0:T(2,128)(2,1)S(1)} %get-tuple-element.9.out, f32[2,46656]{1,0:T(2,128)S(1)} %get-tuple-element.10.ket, f32[2,46656]{1,0:T(2,128)S(1)} %get-tuple-element.11.ket_turned, f32[32,8,128]{2,1,0:T(8,128)S(1)} %get-tuple-element.12.half, ...), custom_call_target="tpu_custom_call" | custom-call | tf_op jit(solution)/shard_map/finish/pallas_call | solution.py:352
